TPU v7x, 32 devices: a whole 2x2x4 slice. The times are simulated.
32 devices in a mesh: batch: 4 (over y, x), tm: 4 (over z), tensor: 2 (over core).
Axes of the slice: x: 2, y: 2, z: 4, core: 2. Of those that a mesh axis runs over, the one named last changes fastest.
Arguments:
- q_raw: bfloat16 [4, 1536, 3072], P('batch', 'tm', 'tensor'), may hold values from -2500 to 2500
- k_raw: bfloat16 [4, 1536, 3072], P('batch', 'tm', 'tensor'), may hold values from -2500 to 2500
- values: bfloat16 [4, 1536, 3072], P('batch', 'tm', 'tensor'), may hold values from -6 to 6
- grad_out: bfloat16 [4, 1536, 3072], P('batch', 'tm', 'tensor'), may hold values from -16 to 16
- gain_q: float32 [3072], P('tensor'), may hold values from 0.25 to 1.75
- gain_k: float32 [3072], P('tensor'), may hold values from 0.25 to 1.75
- tile_lists: int32 [4, 4, 3], P('batch', 'tm'), may hold values from -1 to 3, as said below
Outputs:
- grad_q: bfloat16 [4, 1536, 3072], P('batch', 'tm', 'tensor')
- grad_k: bfloat16 [4, 1536, 3072], P('batch', 'tm', 'tensor')
- grad_values: bfloat16 [4, 1536, 3072], P('batch', 'tm', 'tensor')
- grad_gain_q: float32 [3072], P('tensor')
- grad_gain_k: float32 [3072], P('tensor')
Inputs may be any that keep to these rules, and one draw needn't show every extreme that they name: `tile_lists`: every entry is a key tile or -1 for an empty slot. A list names no tile twice, always names its own query tile, and names only tiles whose time slab (tile) differs from the query tile's by at most one; in every clip some list fills all 3 slots.
All inputs are finite; a program needn't handle non-finite values.
Results may differ from a plain program's by a relative error of at most 0.0107.
The roundings to bfloat16 on the way count: a program that leaves them out, or rounds other values in their place, can miss the bound.
Values may be sent and summed in bfloat16 or wider, within the bound.
A program may use at most 128 MiB of HBM per device.

v0:
```python
import math

import jax
import jax.numpy as jnp
from jax import lax
from jax.sharding import PartitionSpec as P

HD = 128


EPSILON = 1e-06
MASKED_SCORE = -1e30


def padded(shard, sides, width):
    for axis, dim in sides:
        peers, length = (lax.axis_size(axis), shard.shape[dim])
        up = [(i, (i + 1) % peers) for i in range(peers - 1)]
        down = [(j, i) for i, j in up]
        last = lax.slice_in_dim(shard, length - width, length, axis=dim)
        first = lax.slice_in_dim(shard, 0, width, axis=dim)
        before = lax.ppermute(last, axis, up)
        after = lax.ppermute(first, axis, down)
        shard = jnp.concatenate([before, shard, after], axis=dim)
    return shard


def head_slice(source, column):
    return lax.dynamic_slice_in_dim(source, column, HD, source.ndim - 1)


def contract_rows(left_side, right_side):
    return lax.dot_general(
        left_side, right_side, (((0,), (0,)), ((), ())), preferred_element_type=jnp.float32
    )


def contract_cols(left_side, right_side):
    return lax.dot_general(
        left_side, right_side, (((1,), (1,)), ((), ())), preferred_element_type=jnp.float32
    )


def regroup(stacked, picked_count, tile_len):
    head_count = stacked.shape[0]
    return (
        stacked.reshape(head_count, picked_count, tile_len, HD)
        .transpose(1, 2, 0, 3)
        .reshape(picked_count, tile_len, head_count * HD)
    )


def query_tile(query_rows, grad_rows, key_rows, value_rows, live_slots):
    tile_len = query_rows.shape[0]
    slot_count = key_rows.shape[0]
    head_count = query_rows.shape[1] // HD
    score_scale = HD ** (-0.5)
    live_cols = jnp.repeat(live_slots, tile_len)

    def per_head(number):
        column = number * HD
        query_head = head_slice(query_rows, column)
        grad_head = head_slice(grad_rows, column)
        key_head = head_slice(key_rows, column).reshape(slot_count * tile_len, HD)
        value_head = head_slice(value_rows, column).reshape(slot_count * tile_len, HD)
        scores = contract_cols(query_head, key_head) * score_scale
        scores = jnp.where(live_cols[None, :], scores, MASKED_SCORE)
        highest = jnp.max(scores, axis=1, keepdims=True)
        exponent = jnp.exp(scores - highest)
        summed = jnp.sum(exponent, axis=1, keepdims=True)
        attn_probs = exponent / summed
        dprobs = contract_cols(grad_head, value_head)
        row_delta = jnp.sum(attn_probs * dprobs, axis=1, keepdims=True)
        dscore = (attn_probs * (dprobs - row_delta)).astype(jnp.bfloat16)
        probs_b = attn_probs.astype(jnp.bfloat16)
        grad_query = jnp.dot(dscore, key_head, preferred_element_type=jnp.float32) * score_scale
        grad_key = contract_rows(dscore, query_head) * score_scale
        grad_value = contract_rows(probs_b, grad_head)
        return (
            grad_query,
            grad_key,
            grad_value,
            highest[:, 0] + jnp.log(summed[:, 0]),
            row_delta[:, 0],
        )

    grad_query, grad_key, grad_value, log_total, row_delta = lax.map(
        per_head, jnp.arange(head_count)
    )
    grad_query = grad_query.transpose(1, 0, 2).reshape(tile_len, head_count * HD)
    grad_pair = jnp.stack(
        [regroup(grad_key, slot_count, tile_len), regroup(grad_value, slot_count, tile_len)]
    )
    return (grad_query, grad_pair, log_total, row_delta)


def finish_norm(wide_rows, inverse, gain_row, grad_normed, projection, feature_count):
    cubed = inverse * inverse * inverse
    grad_rows = (
        inverse[:, None] * gain_row[None, :] * grad_normed
        - wide_rows * (cubed * projection / feature_count)[:, None]
    )
    return grad_rows.astype(jnp.bfloat16)


def shards(q_raw, k_raw, values, grad_out, gain_q, gain_k, tile_lists):
    query_wide = q_raw[0].astype(jnp.float32)
    key_wide = k_raw[0].astype(jnp.float32)
    value_rows = values[0]
    grad_rows = grad_out[0]
    tile_rows = tile_lists[0]
    token_count, feature_count = query_wide.shape
    tiles_here, slot_count = tile_rows.shape
    tile_len = token_count // tiles_here
    width_all = feature_count * lax.axis_size("tensor")
    count_all = lax.axis_size("batch") * lax.axis_size("tm") * token_count
    squares = lax.psum(
        (jnp.sum(query_wide * query_wide, axis=1), jnp.sum(key_wide * key_wide, axis=1)), "tensor"
    )
    inverse_q = lax.rsqrt(squares[0] / width_all + EPSILON)
    inverse_k = lax.rsqrt(squares[1] / width_all + EPSILON)
    query_norm = (query_wide * inverse_q[:, None] * gain_q[None, :]).astype(jnp.bfloat16)
    key_norm = (key_wide * inverse_k[:, None] * gain_k[None, :]).astype(jnp.bfloat16)
    position = lax.axis_index("tm")
    nearby = padded(jnp.stack([key_norm, value_rows]), (("tm", 1),), token_count)
    nearby = nearby.reshape(2, 3 * tiles_here, tile_len, feature_count)
    first_tile = (position - 1) * tiles_here
    grad_buffer = jnp.zeros((2, 3 * tiles_here, tile_len, feature_count), jnp.float32)
    entries = tile_rows[0]
    places = jnp.clip(entries - first_tile, 0, 3 * tiles_here - 1)
    grad_query, grad_pair, log_total, row_delta = query_tile(
        query_norm, grad_rows, nearby[0][places], nearby[1][places], entries >= 0
    )
    grad_buffer = grad_buffer.at[:, places].add(grad_pair)
    outer_parts = jnp.stack([grad_buffer[:, :tiles_here], grad_buffer[:, 2 * tiles_here :]])
    returned = padded(outer_parts.astype(jnp.bfloat16), (("tm", 0),), 1).astype(outer_parts.dtype)
    own_grads = grad_buffer[:, tiles_here : 2 * tiles_here] + returned[0] + returned[3]
    grad_kn = own_grads[0].reshape(token_count, feature_count)
    grad_values = own_grads[1].reshape(token_count, feature_count).astype(jnp.bfloat16)
    local_q = jnp.sum(query_wide * gain_q[None, :] * grad_query, axis=1)
    local_k = jnp.sum(key_wide * gain_k[None, :] * grad_kn, axis=1)
    proj_q = lax.psum(local_q, "tensor")
    proj_k = lax.psum(local_k, "tensor")
    grad_q = finish_norm(query_wide, inverse_q, gain_q, grad_query, proj_q, width_all)
    grad_k = finish_norm(key_wide, inverse_k, gain_k, grad_kn, proj_k, width_all)
    gain_terms = lax.psum(
        (
            jnp.sum(grad_query * query_wide * inverse_q[:, None], axis=0),
            jnp.sum(grad_kn * key_wide * inverse_k[:, None], axis=0),
        ),
        ("batch", "tm"),
    )
    factor_all = 1.0 / math.sqrt(count_all)
    return (
        grad_q[None],
        grad_k[None],
        grad_values[None],
        gain_terms[0] * factor_all,
        gain_terms[1] * factor_all,
    )


def solution(mesh):
    placed = (
        P("batch", "tm", "tensor"),
        P("batch", "tm", "tensor"),
        P("batch", "tm", "tensor"),
        P("batch", "tm", "tensor"),
        P("tensor"),
        P("tensor"),
        P("batch", "tm", None),
    )
    return jax.shard_map(
        shards,
        mesh=mesh,
        in_specs=placed,
        out_specs=(
            P("batch", "tm", "tensor"),
            P("batch", "tm", "tensor"),
            P("batch", "tm", "tensor"),
            P("tensor"),
            P("tensor"),
        ),
        check_vma=False,
    )
```

profile of v0, /device:TPU:0, one launch (start us, length us, event | category | flops | bytes accessed | tf_op | source)
XLA Modules:
  0.0 473.5 jit_solution(5523709214736830723)
XLA Ops:
  3.1 2.6 all-reduce.2
  7.1 2.9 pad_maximum_fusion.1
  10.0 6.2 %collective-permute-start = (bf16[2,384,1536]{2,1,0:T(8,128)(2,1)}, bf16[2,384,1536]{2,1,0:T(8,128)(2,1)}, u32[]{:S(2)}, u32[]{:S(2)}) collective-permute-start(bf16[2,384,1536]{2,1,0:T(8,128)(2,1)} %pad_maximum_fusion.1), channel_id=1, source_target_pairs={{0,2},{2,4},{4,6},{1,3},{3,5},{5,7},{8,10},{10,12},{12,14},{9,11},... | collective-permute-start | bytes 7077896 | tf_op jit(solution)/shard_map/ppermute | solution.py:22
  18.9 47.0 %collective-permute-done = bf16[2,384,1536]{2,1,0:T(8,128)(2,1)} collective-permute-done((bf16[2,384,1536]{2,1,0:T(8,128)(2,1)}, bf16[2,384,1536]{2,1,0:T(8,128)(2,1)}, u32[]{:S(2)}, u32[]{:S(2)}) %collective-permute-start) | collective-permute-done | bytes 2359328 | tf_op jit(solution)/shard_map/ppermute | solution.py:22
  65.9 5.5 %collective-permute-done.1 = bf16[2,384,1536]{2,1,0:T(8,128)(2,1)} collective-permute-done((bf16[2,384,1536]{2,1,0:T(8,128)(2,1)}, bf16[2,384,1536]{2,1,0:T(8,128)(2,1)}, u32[]{:S(2)}, u32[]{:S(2)}) %collective-permute-start.1) | collective-permute-done | bytes 2359328 | tf_op jit(solution)/shard_map/ppermute | solution.py:23
  71.4 3.7 pad_maximum_fusion
  75.1 3.3 fusion.55
  78.4 4.6 gather_fusion
  83.0 4.6 gather_fusion.1
  87.7 146.1 %while.15 = (s32[]{:T(128)}, f32[12,384,128]{1,2,0:T(8,128)}, f32[12,1152,128]{2,1,0:T(8,128)}, f32[12,1152,128]{2,1,0:T(8,128)}, s32[12]{0:T(128)S(1)}, /*index...) while((s32[]{:T(128)}, f32[12,384,128]{1,2,0:T(8,128)}, ...), condition=%wide.region_8.9_spmd.clone, body=%wide.region_4.8_spmd.clone.sunk | while | flops 573946752 | bytes 19684052 | solution.py:87
  92.0 2.4 fusion.86
  96.4 2.2 fusion.85
  104.2 2.4 fusion.86
  108.6 2.2 fusion.85
  116.3 2.5 fusion.86
  120.8 2.2 fusion.85
  128.5 2.5 fusion.86
  133.0 2.2 fusion.85
  140.8 2.4 fusion.86
  145.2 2.2 fusion.85
  152.9 2.4 fusion.86
  157.3 2.2 fusion.85
  165.1 2.4 fusion.86
  169.5 2.2 fusion.85
  177.3 2.4 fusion.86
  181.7 2.2 fusion.85
  189.4 2.4 fusion.86
  193.8 2.2 fusion.85
  201.6 2.4 fusion.86
  206.0 2.2 fusion.85
  213.8 2.5 fusion.86
  218.2 2.2 fusion.85
  226.0 2.4 fusion.86
  230.4 2.2 fusion.85
  233.8 8.1 %copy.32 = f32[3,384,12,128]{1,3,2,0:T(8,128)} copy(f32[3,384,12,128]{3,1,0,2:T(8,128)} %bitcast.160) | data formatting | bytes 14155776 | tf_op jit(solution)/shard_map/transpose | solution.py:48
  241.9 8.1 %copy.33 = f32[3,384,12,128]{1,3,2,0:T(8,128)} copy(f32[3,384,12,128]{3,1,0,2:T(8,128)} %bitcast.161) | data formatting | bytes 14155776 | tf_op jit(solution)/shard_map/transpose | solution.py:48
  250.0 11.0 %maximum_bitcast_fusion = f32[3,2,384,1536]{2,3,0,1:T(8,128)} fusion(f32[1,3,384,1536]{2,3,1,0:T(8,128)} %bitcast.155, f32[1,3,384,1536]{2,3,1,0:T(8,128)} %bitcast.154), kind=kLoop, calls=%fused_computation.31 | loop fusion | flops 3538944 | bytes 28311552 | tf_op jit(solution)/shard_map/stack | solution.py:91
  260.9 15.3 %copy.34 = f32[3,2,384,1536]{3,2,1,0:T(8,128)} copy(f32[3,2,384,1536]{2,3,0,1:T(8,128)} %maximum_bitcast_fusion) | data formatting | bytes 28311552 | tf_op jit(solution)/shard_map/stack | solution.py:91
  276.3 6.8 %broadcast_in_dim.36 = f32[2,3,384,1536]{3,2,1,0:T(8,128)} broadcast(f32[]{:T(128)} %constant.11.clone.1), dimensions={} | broadcast | bytes 14155780 | tf_op jit(solution)/shard_map/broadcast_in_dim | solution.py:128
  283.1 19.9 %scatter_fusion = f32[2,3,384,1536]{3,2,1,0:T(8,128)} fusion(f32[2,3,384,1536]{3,2,1,0:T(8,128)} %broadcast_in_dim.36, s32[3]{0:T(128)S(1)} %fusion.52, f32[3,2,384,1536]{3,2,1,0:T(8,128)} %copy.34), kind=kCustom, calls=%fused_computation.2 | custom fusion | flops 3538944 | bytes 42467340 | tf_op jit(solution)/shard_map/scatter-add | solution.py:134
  303.0 6.9 %fusion.45 = (bf16[1,2,1,384,1536]{4,3,1,0,2:T(8,128)(2,1)}, bf16[1,2,1,384,1536]{4,3,1,2,0:T(8,128)(2,1)}, bf16[1,2,384,1536]{3,2,1,0:T(8,128)(2,1)S(1)}, bf16[1,2,384,1536]{3,2,1,0:T(8,128)(2,1)S(1)}) fusion(f32[2,3,384,1536]{3,2,1,0:T(8,128)} %scatter_fusion), kind=kLoop, calls=%fused_computation.76 | loop fusion | bytes 14155776 | tf_op jit(solution)/shard_map/stack | solution.py:135
  311.2 4.9 %collective-permute-start.2 = (bf16[1,2,1,384,1536]{4,3,1,0,2:T(8,128)(2,1)}, bf16[1,2,1,384,1536]{4,3,1,0,2:T(8,128)(2,1)S(1)}, u32[]{:S(2)}, u32[]{:S(2)}) collective-permute-start(bf16[1,2,1,384,1536]{4,3,1,0,2:T(8,128)(2,1)} %get-tuple-element.151), channel_id=1, source_target_pairs={{0,2},{2,4},{4,6},{1,3},{3,5},{5,7},{8,10},{10,12},{12,14},{9,11},... | collective-permute-start | bytes 7077896 | tf_op jit(solution)/shard_map/ppermute | solution.py:22
  317.4 46.8 %collective-permute-done.3 = bf16[1,2,1,384,1536]{4,3,1,2,0:T(8,128)(2,1)S(1)} collective-permute-done((bf16[1,2,1,384,1536]{4,3,1,2,0:T(8,128)(2,1)}, bf16[1,2,1,384,1536]{4,3,1,2,0:T(8,128)(2,1)S(1)}, u32[]{:S(2)}, u32[]{:S(2)}) %collective-permute-start.3) | collective-permute-done | bytes 2359328 | tf_op jit(solution)/shard_map/ppermute | solution.py:23
  365.5 12.8 %fusion.53 = (f32[4,2,1,384,1536]{4,3,1,2,0:T(8,128)}, f32[4,2,1,384,1536]{4,3,1,0,2:T(8,128)}) fusion(bf16[1,2,1,384,1536]{4,3,1,0,2:T(8,128)(2,1)S(1)} %bitcast.162, bf16[2,2,1,384,1536]{4,3,1,0,2:T(8,128)(2,1)S(1)} %maximum_bitcast_fusion.1, bf16[1,2,1,384,1536]{4,3,1,0,2:T(8,128)(2,1)S(1)} %collective-permute-done.2), kind=kLoop, calls=%fused_computation.93 | loop fusion | flops 14155776 | bytes 47185920 | tf_op jit(solution)/shard_map/convert_element_type | solution.py:136
  378.3 6.7 %fusion.20 = f32[2,1,384,1536]{3,2,0,1:T(8,128)S(1)} fusion(f32[4,2,1,384,1536]{4,3,1,0,2:T(8,128)} %get-tuple-element.156, f32[4,2,1,384,1536]{4,3,1,2,0:T(8,128)} %get-tuple-element.155, f32[2,3,384,1536]{3,2,1,0:T(8,128)} %scatter_fusion), kind=kLoop, calls=%fused_computation.35 | loop fusion | flops 2359296 | bytes 18874368 | tf_op jit(solution)/shard_map/add | solution.py:137
  387.5 77.0 %all-reduce = (f32[1536]{0:T(1024)S(1)}, f32[1536]{0:T(1024)S(1)}) all-reduce(f32[1536]{0:T(1024)S(1)} %bitcast.164, f32[1536]{0:T(1024)S(1)} %get-tuple-element.115), channel_id=1, replica_groups=mesh['batch'=4,'tm'=4,'tensor'=2] {'batch','tm'}, use_global_device_ids=true, to_apply=%region_15.16 | all-reduce | flops 3072 | bytes 24576 | tf_op jit(solution)/shard_map/psum | solution.py:146
  465.7 2.4 all-reduce.1
  468.2 3.3 fusion.34
  (176 shorter events, 98.8 us)
Async XLA Ops:
  0.6 2.1 copy-start.1
  0.6 5.1 %copy-start.6 = (f32[1536]{0:T(1024)S(1)}, f32[1536]{0:T(1024)}, u32[]{:S(2)}) copy-start(f32[1536]{0:T(1024)} %param.14) | copy-start | bytes 18436
  6.1 1.0 copy-start.2
  7.1 10.4 %copy-start.8 = (s32[1,1,3]{2,1,0:T(1,128)S(1)}, s32[1,1,3]{2,1,0:T(1,128)}, u32[]{:S(2)}) copy-start(s32[1,1,3]{2,1,0:T(1,128)} %param.15) | copy-start | bytes 40
  7.1 10.5 %copy-start.7 = (f32[1536]{0:T(1024)S(1)}, f32[1536]{0:T(1024)}, u32[]{:S(2)}) copy-start(f32[1536]{0:T(1024)} %param.13) | copy-start | bytes 18436
  10.0 55.9 %collective-permute-start = (bf16[2,384,1536]{2,1,0:T(8,128)(2,1)}, bf16[2,384,1536]{2,1,0:T(8,128)(2,1)}, u32[]{:S(2)}, u32[]{:S(2)}) collective-permute-start(bf16[2,384,1536]{2,1,0:T(8,128)(2,1)} %pad_maximum_fusion.1), channel_id=1, source_target_pairs={{0,2},{2,4},{4,6},{1,3},{3,5},{5,7},{8,10},{10,12},{12,14},{9,11},... | collective-permute-start | bytes 7077896 | tf_op jit(solution)/shard_map/ppermute | solution.py:22
  16.2 55.2 %collective-permute-start.1 = (bf16[2,384,1536]{2,1,0:T(8,128)(2,1)}, bf16[2,384,1536]{2,1,0:T(8,128)(2,1)}, u32[]{:S(2)}, u32[]{:S(2)}) collective-permute-start(bf16[2,384,1536]{2,1,0:T(8,128)(2,1)} %pad_maximum_fusion.1), channel_id=1, source_target_pairs={{2,0},{4,2},{6,4},{3,1},{5,3},{7,5},{10,8},{12,10},{14,12},{11,9},... | collective-permute-start | bytes 7077896 | tf_op jit(solution)/shard_map/ppermute | solution.py:23
  17.5 53.9 %copy-start.3 = (bf16[1,384,1536]{2,1,0:T(8,128)(2,1)S(1)}, bf16[1,384,1536]{2,1,0:T(8,128)(2,1)}, u32[]{:S(2)}) copy-start(bf16[1,384,1536]{2,1,0:T(8,128)(2,1)} %copy-done.2) | copy-start | bytes 3538948
  303.0 13.1 %copy-start.4 = (f32[12,384,128]{1,2,0:T(8,128)S(1)}, f32[12,384,128]{1,2,0:T(8,128)}, u32[]{:S(2)}) copy-start(f32[12,384,128]{1,2,0:T(8,128)} %get-tuple-element.59) | copy-start | bytes 7077892
  309.9 54.3 %collective-permute-start.3 = (bf16[1,2,1,384,1536]{4,3,1,2,0:T(8,128)(2,1)}, bf16[1,2,1,384,1536]{4,3,1,2,0:T(8,128)(2,1)S(1)}, u32[]{:S(2)}, u32[]{:S(2)}) collective-permute-start(bf16[1,2,1,384,1536]{4,3,1,2,0:T(8,128)(2,1)} %get-tuple-element.152), channel_id=1, source_target_pairs={{2,0},{4,2},{6,4},{3,1},{5,3},{7,5},{10,8},{12,10},{14,12},{11,9},... | collective-permute-start | bytes 7077896 | tf_op jit(solution)/shard_map/ppermute | solution.py:23
  311.2 54.3 %collective-permute-start.2 = (bf16[1,2,1,384,1536]{4,3,1,0,2:T(8,128)(2,1)}, bf16[1,2,1,384,1536]{4,3,1,0,2:T(8,128)(2,1)S(1)}, u32[]{:S(2)}, u32[]{:S(2)}) collective-permute-start(bf16[1,2,1,384,1536]{4,3,1,0,2:T(8,128)(2,1)} %get-tuple-element.151), channel_id=1, source_target_pairs={{0,2},{2,4},{4,6},{1,3},{3,5},{5,7},{8,10},{10,12},{12,14},{9,11},... | collective-permute-start | bytes 7077896 | tf_op jit(solution)/shard_map/ppermute | solution.py:22
  385.0 2.5 copy-start
  468.2 3.4 copy-start.5
where the time goes:
time: 476 us; the launch traced here: 474 us
  waiting for transfers between devices  101 us (21%)
  matrix products  95.5 us (20%)
  local copies, waits for them, and re-layouts  95.2 us (20%)
  blocking collectives  82.1 us (17%)
  other arithmetic  77.5 us (16%)
  starting transfers between devices  13.6 us (3%)
  loops' own time  8.21 us (2%)
    psum x1, blocking collectives, shards(): lax.psum((jnp.sum(grad_query * query_wide * inverse_q[:, None], axis=0),...  77 us
    dot_general x24, matrix products, contract_rows(): lax.dot_general(left_side, right_side, (((0,), (0,)), ((), ())), preferre...  55.1 us
    ppermute x2, waiting for transfers between devices, padded(): after = lax.ppermute(first, axis, down)  52.3 us
    ppermute x2, waiting for transfers between devices, padded(): before = lax.ppermute(last, axis, up)  48.3 us
    dot_general x24, matrix products, contract_cols(): lax.dot_general(left_side, right_side, (((1,), (1,)), ((), ())), preferre...  35.6 us
    scatter-add x1, other arithmetic, shards(): grad_buffer = grad_buffer.at[:, places].add(grad_pair)  19.9 us
    transpose x2, local copies, waits for them, and re-layouts, regroup(): return stacked.reshape(head_count, picked_count, tile_len, HD).transpose(...  16.2 us
    another operation x1, local copies, waits for them, and re-layouts, query_tile(): jnp.stack([regroup(grad_key, slot_count, tile_len), regroup(grad_value, s...  15.3 us
  transfers between devices with their start and end apart: 4, of which 4 were waited for; matrix products, arithmetic and copies ran while one was open for 1% of the time, Pallas kernels for 0%

commit v1 on v0

v1 whole, which is shorter than its diff:
```python
import math

import jax
import jax.numpy as jnp
from jax import lax
from jax.experimental import pallas as pl
from jax.experimental.pallas import tpu as pltpu
from jax.sharding import PartitionSpec as P

HD = 128
STATS = 4
EPSILON = 1e-06
DEAD = 1e30
SCALE = HD ** (-0.5)
CHUNKS = 3


def cols_dot(left, right):
    return lax.dot_general(
        left, right, (((1,), (1,)), ((), ())), preferred_element_type=jnp.float32
    )


def rows_dot(left, right):
    return lax.dot_general(
        left, right, (((0,), (0,)), ((), ())), preferred_element_type=jnp.float32
    )


def stats_body(count, *refs):
    key = refs[0][...]
    value = refs[1][...]
    for t in range(count):
        query = refs[2 + t][...]
        grad = refs[2 + count + t][...]
        out = refs[2 + 2 * count + t]
        scores = cols_dot(key, query) * SCALE
        highest = jnp.max(scores, axis=0, keepdims=True)
        exponent = jnp.exp(scores - highest)
        dprobs = cols_dot(value, grad)
        out[0, 0:1, :] = highest
        out[0, 1:2, :] = jnp.sum(exponent, axis=0, keepdims=True)
        out[0, 2:3, :] = jnp.sum(exponent * dprobs, axis=0, keepdims=True)
        out[0, 3:4, :] = jnp.zeros_like(highest)


def partial_stats(key, value, queries, grads):
    rows, width = key.shape
    heads = width // HD
    count = len(queries)
    column = pl.BlockSpec((rows, HD), lambda h: (0, h))
    stat = pl.BlockSpec((1, STATS, rows), lambda h: (h, 0, 0))

    def body(*refs):
        stats_body(count, *refs)

    return pl.pallas_call(
        body,
        grid=(heads,),
        out_shape=[jax.ShapeDtypeStruct((heads, STATS, rows), jnp.float32)] * count,
        in_specs=[column] * (2 + 2 * count),
        out_specs=[stat] * count,
        cost_estimate=pl.CostEstimate(
            flops=4 * count * rows * rows * width,
            bytes_accessed=(2 + 2 * count) * rows * width * 2,
            transcendentals=count * rows * rows * heads,
        ),
        name=f"stats{count}",
    )(key, value, *queries, *grads)


def combine_body(live, own, before, after, to_own, to_before, to_after):
    alive = (live[0] > 0, live[1] > 0)
    highest = own[:, 0:1, :]
    parts = (before, after)
    for flag, part in zip(alive, parts):
        highest = jnp.where(flag, jnp.maximum(highest, part[:, 0:1, :]), highest)
    weight = jnp.exp(own[:, 0:1, :] - highest)
    total = weight * own[:, 1:2, :]
    delta = weight * own[:, 2:3, :]
    for flag, part in zip(alive, parts):
        weight = jnp.exp(jnp.minimum(part[:, 0:1, :] - highest, 0.0))
        total = total + jnp.where(flag, weight * part[:, 1:2, :], 0.0)
        delta = delta + jnp.where(flag, weight * part[:, 2:3, :], 0.0)
    inverse = 1.0 / total
    delta = delta * inverse
    for out in (to_own, to_before, to_after):
        out[:, 1:2, :] = inverse
        out[:, 2:3, :] = delta
        out[:, 3:4, :] = jnp.zeros_like(delta)
    to_own[:, 0:1, :] = highest
    for flag, out in zip(alive, (to_before, to_after)):
        out[:, 0:1, :] = jnp.where(flag, highest, DEAD)


def combine(live, own, before, after):
    whole = pl.BlockSpec(memory_space=pltpu.VMEM)
    return pl.pallas_call(
        combine_body,
        out_shape=[jax.ShapeDtypeStruct(own.shape, own.dtype)] * 3,
        in_specs=[pl.BlockSpec(memory_space=pltpu.SMEM), whole, whole, whole],
        out_specs=[whole] * 3,
        name="combine",
    )(live, own, before, after)


def grads_body(key_ref, value_ref, q0, q1, q2, g0, g1, g2, c0, c1, c2,
               dkey, dvalue, dq0, dq1, dq2):
    key = key_ref[...]
    value = value_ref[...]
    key_total = None
    value_total = None
    for query_ref, grad_ref, stat, out in (
        (q0, g0, c0, dq0), (q1, g1, c1, dq1), (q2, g2, c2, dq2)
    ):
        query = query_ref[...]
        grad = grad_ref[...]
        scores = cols_dot(key, query) * SCALE
        probs = jnp.exp(scores - stat[0, 0:1, :]) * stat[0, 1:2, :]
        dprobs = cols_dot(value, grad)
        dscore = (probs * (dprobs - stat[0, 2:3, :])).astype(jnp.bfloat16)
        probs_b = probs.astype(jnp.bfloat16)
        value_term = jnp.dot(probs_b, grad, preferred_element_type=jnp.float32)
        key_term = jnp.dot(dscore, query, preferred_element_type=jnp.float32)
        value_total = value_term if value_total is None else value_total + value_term
        key_total = key_term if key_total is None else key_total + key_term
        out[...] = (rows_dot(key, dscore).T * SCALE).astype(out.dtype)
    dkey[...] = key_total * SCALE
    dvalue[...] = value_total.astype(dvalue.dtype)


def full_grads(key, value, queries, grads, stats, first, heads):
    rows = key.shape[0]
    column = pl.BlockSpec((rows, HD), lambda h: (0, h + first))
    result = pl.BlockSpec((rows, HD), lambda h: (0, h))
    stat = pl.BlockSpec((1, STATS, rows), lambda h: (h + first, 0, 0))
    width = heads * HD

    def shape(dtype):
        return jax.ShapeDtypeStruct((rows, width), dtype)

    return pl.pallas_call(
        grads_body,
        grid=(heads,),
        out_shape=[
            shape(jnp.float32), shape(jnp.bfloat16), shape(jnp.float32),
            shape(jnp.bfloat16), shape(jnp.bfloat16),
        ],
        in_specs=[column] * 8 + [stat] * 3,
        out_specs=[result] * 5,
        cost_estimate=pl.CostEstimate(
            flops=30 * rows * rows * width,
            bytes_accessed=15 * rows * width * 2,
            transcendentals=3 * rows * rows * heads,
        ),
        name="grads",
    )(key, value, *queries, *grads, *stats)


def finish_norm(wide_rows, inverse, gain_row, grad_normed, projection, feature_count):
    cubed = inverse * inverse * inverse
    grad_rows = (
        inverse[:, None] * gain_row[None, :] * grad_normed
        - wide_rows * (cubed * projection / feature_count)[:, None]
    )
    return grad_rows.astype(jnp.bfloat16)


def shards(q_raw, k_raw, values, grad_out, gain_q, gain_k, tile_lists):
    query_wide = q_raw[0].astype(jnp.float32)
    key_wide = k_raw[0].astype(jnp.float32)
    value_rows = values[0]
    grad_rows = grad_out[0]
    entries = tile_lists[0, 0]
    token_count, feature_count = query_wide.shape
    head_count = feature_count // HD
    width_all = feature_count * lax.axis_size("tensor")
    count_all = lax.axis_size("batch") * lax.axis_size("tm") * token_count
    peers = lax.axis_size("tm")
    up = [(i, i + 1) for i in range(peers - 1)]
    down = [(i + 1, i) for i in range(peers - 1)]

    def shift(to_before, to_after):
        return lax.ppermute(to_after, "tm", up), lax.ppermute(to_before, "tm", down)

    grad_before, grad_after = shift(grad_rows, grad_rows)
    squares = lax.psum(
        (jnp.sum(query_wide * query_wide, axis=1), jnp.sum(key_wide * key_wide, axis=1)), "tensor"
    )
    inverse_q = lax.rsqrt(squares[0] / width_all + EPSILON)
    inverse_k = lax.rsqrt(squares[1] / width_all + EPSILON)
    query_norm = (query_wide * inverse_q[:, None] * gain_q[None, :]).astype(jnp.bfloat16)
    key_norm = (key_wide * inverse_k[:, None] * gain_k[None, :]).astype(jnp.bfloat16)
    query_before, query_after = shift(query_norm, query_norm)
    position = lax.axis_index("tm")
    live = jnp.stack(
        [
            jnp.any((entries >= 0) & (entries == position - 1)),
            jnp.any((entries >= 0) & (entries == position + 1)),
        ]
    ).astype(jnp.int32)

    (own,) = partial_stats(key_norm, value_rows, [query_norm], [grad_rows])
    for_before, for_after = partial_stats(
        key_norm, value_rows, [query_before, query_after], [grad_before, grad_after]
    )
    from_before, from_after = shift(for_before, for_after)
    stat_own, to_before, to_after = combine(live, own, from_before, from_after)
    stat_before, stat_after = shift(to_before, to_after)

    chunks = math.gcd(CHUNKS, head_count)
    heads = head_count // chunks
    key_parts, value_parts, query_parts = [], [], []
    for chunk in range(chunks):
        dkey, dvalue, own_dq, before_dq, after_dq = full_grads(
            key_norm,
            value_rows,
            [query_norm, query_before, query_after],
            [grad_rows, grad_before, grad_after],
            [stat_own, stat_before, stat_after],
            chunk * heads,
            heads,
        )
        back_before, back_after = shift(before_dq, after_dq)
        key_parts.append(dkey)
        value_parts.append(dvalue)
        query_parts.append(
            own_dq + back_before.astype(jnp.float32) + back_after.astype(jnp.float32)
        )
    grad_kn = jnp.concatenate(key_parts, axis=1)
    grad_values = jnp.concatenate(value_parts, axis=1)
    grad_query = jnp.concatenate(query_parts, axis=1)

    local_q = jnp.sum(query_wide * gain_q[None, :] * grad_query, axis=1)
    local_k = jnp.sum(key_wide * gain_k[None, :] * grad_kn, axis=1)
    proj_k = lax.psum(local_k, "tensor")
    proj_q = lax.psum(local_q, "tensor")
    grad_q = finish_norm(query_wide, inverse_q, gain_q, grad_query, proj_q, width_all)
    grad_k = finish_norm(key_wide, inverse_k, gain_k, grad_kn, proj_k, width_all)
    gain_terms = lax.psum(
        (
            jnp.sum(grad_query * query_wide * inverse_q[:, None], axis=0),
            jnp.sum(grad_kn * key_wide * inverse_k[:, None], axis=0),
        ),
        ("batch", "tm"),
    )
    factor_all = 1.0 / math.sqrt(count_all)
    return (
        grad_q[None],
        grad_k[None],
        grad_values[None],
        gain_terms[0] * factor_all,
        gain_terms[1] * factor_all,
    )


def solution(mesh):
    rows = P("batch", "tm", "tensor")
    return jax.shard_map(
        shards,
        mesh=mesh,
        in_specs=(rows, rows, rows, rows, P("tensor"), P("tensor"), P("batch", "tm", None)),
        out_specs=(rows, rows, rows, P("tensor"), P("tensor")),
        check_vma=False,
    )
```

time: 476 us -> 251 us (0.53)
  matrix products: 95.5 us -> 0 us
  local copies, waits for them, and re-layouts: 95.2 us -> 5.34 us
  other arithmetic: 77.5 us -> 19.7 us
  waiting for transfers between devices: 101 us -> 49.5 us
  Pallas kernels: 0 us -> 48.9 us
  starting transfers between devices: 13.6 us -> 42.8 us
  loops' own time: 8.21 us -> 0 us
    dot_general x60 -> x0, matrix products: 95.5 us -> none  [the longest x24 55.1 us: contract_rows(): lax.dot_general(left_side, right_side, (((0,), (0,)), ((), ())), preferre...]
    ppermute x4 -> x14, waiting for transfers between devices: 101 us -> 49.5 us  [the longest x7 34.6 us: shift(): lax.ppermute(to_after, 'tm', up)]
    pallas_call x0 -> x6, Pallas kernels: none -> 48.9 us  [the longest x3 25 us: full_grads(): pl.pallas_call(grads_body, grid=(heads,), out_shape=[shape(jnp.float32),...]
    ppermute x4 -> x14, starting transfers between devices: 13.6 us -> 42.8 us  [the longest x7 33.6 us: shift(): lax.ppermute(to_after, 'tm', up)]
    another operation x2 -> x0, local copies, waits for them, and re-layouts: 22.3 us -> none  [the longest x1 15.3 us: query_tile(): jnp.stack([regroup(grad_key, slot_count, tile_len), regroup(grad_value, s...]
    dynamic_slice x24 -> x0, local copies, waits for them, and re-layouts: 20.2 us -> none  [the longest x12 13.3 us: head_slice(): return lax.dynamic_slice_in_dim(source, column, HD, source.ndim - 1)]
    scatter-add x1 -> x0, other arithmetic: 19.9 us -> none  [shards(): grad_buffer = grad_buffer.at[:, places].add(grad_pair)]
    convert_element_type x13 -> x1, other arithmetic: 18.7 us -> 1.88 us  [shards(): live = jnp.stack([jnp.any((entries >= 0) & (entries == position - 1)), jn...]
  transfers between devices with their start and end apart: 4 -> 14, of which waited for: 4 -> 7; matrix products, arithmetic and copies ran while one was open for 1% -> 5% of each run, Pallas kernels for 0% -> 11%
where the time goes in v1:
time: 251 us; the launch traced here: 249 us
  blocking collectives  81.7 us (33%)
  waiting for transfers between devices  49.5 us (20%)
  Pallas kernels  48.9 us (19%)
  starting transfers between devices  42.8 us (17%)
  other arithmetic  19.7 us (8%)
  local copies, waits for them, and re-layouts  5.34 us (2%)
    psum x1, blocking collectives, shards(): lax.psum((jnp.sum(grad_query * query_wide * inverse_q[:, None], axis=0),...  76.1 us
    ppermute x7, waiting for transfers between devices, shift(): lax.ppermute(to_after, 'tm', up)  34.6 us
    ppermute x7, starting transfers between devices, shift(): lax.ppermute(to_after, 'tm', up)  33.6 us
    pallas_call x3, Pallas kernels, full_grads(): pl.pallas_call(grads_body, grid=(heads,), out_shape=[shape(jnp.float32),...  25 us
    pallas_call x2, Pallas kernels, partial_stats(): pl.pallas_call(body, grid=(heads,), out_shape=[jax.ShapeDtypeStruct((head...  22.1 us
    ppermute x7, waiting for transfers between devices, shift(): lax.ppermute(to_before, 'tm', down)  14.9 us
    ppermute x7, starting transfers between devices, shift(): lax.ppermute(to_before, 'tm', down)  9.15 us
    unnamed x66, local copies, waits for them, and re-layouts  5.29 us
  transfers between devices with their start and end apart: 14, of which 7 were waited for; matrix products, arithmetic and copies ran while one was open for 5% of the time, Pallas kernels for 11%

profile of v1, /device:TPU:0, one launch (start us, length us, event | category | flops | bytes accessed | tf_op | source)
XLA Modules:
  0.0 249.0 jit_solution(12057901245775569183)
XLA Ops:
  0.7 1.7 fusion.17
  2.4 1.6 fusion.8
  4.0 3.2 %all-reduce.2 = (f32[384]{0:T(512)}, f32[384]{0:T(512)S(1)}) all-reduce(f32[384]{0:T(512)S(1)} %fusion.17, f32[384]{0:T(512)S(1)} %fusion.8), channel_id=1, replica_groups=mesh['batch'=4,'tm'=4,'tensor'=2] {'tensor'}, use_global_device_ids=true, to_apply=%region_3.0 | all-reduce | flops 768 | bytes 6144 | tf_op jit(solution)/shard_map/psum | solution.py:187
  8.3 5.9 %collective-permute-start = (bf16[384,1536]{1,0:T(8,128)(2,1)S(1)}, bf16[384,1536]{1,0:T(8,128)(2,1)}, u32[]{:S(2)}, u32[]{:S(2)}) collective-permute-start(bf16[384,1536]{1,0:T(8,128)(2,1)S(1)} %fusion.10.refs_2_.q0), channel_id=1, source_target_pairs={{0,2},{2,4},{4,6},{1,3},{3,5},{5,7},{8,10},{10,12},{12,14},{9,11},... | collective-permute-start | bytes 3538952 | tf_op jit(solution)/shard_map/ppermute | solution.py:184
  14.2 1.3 collective-permute-start.1
  15.4 5.6 %collective-permute-start.2 = (bf16[384,1536]{1,0:T(8,128)(2,1)}, bf16[384,1536]{1,0:T(8,128)(2,1)}, u32[]{:S(2)}, u32[]{:S(2)}) collective-permute-start(bf16[384,1536]{1,0:T(8,128)(2,1)} %bitcast.3.refs_3_.g0), channel_id=1, source_target_pairs={{0,2},{2,4},{4,6},{1,3},{3,5},{5,7},{8,10},{10,12},{12,14},{9,11},... | collective-permute-start | bytes 3538952 | tf_op jit(solution)/shard_map/ppermute | solution.py:184
  21.0 1.3 collective-permute-start.3
  22.3 1.3 and_reduce_fusion.1
  23.6 1.9 add_convert_fusion.live
  25.5 0.7 add_rsqrt_fusion
  26.2 1.4 fusion.19.refs_0_.key_ref
  27.6 11.9 %collective-permute-done.refs_2_.q1 = bf16[384,1536]{1,0:T(8,128)(2,1)} collective-permute-done((bf16[384,1536]{1,0:T(8,128)(2,1)S(1)}, bf16[384,1536]{1,0:T(8,128)(2,1)}, u32[]{:S(2)}, u32[]{:S(2)}) %collective-permute-start) | collective-permute-done | bytes 1179680 | tf_op jit(solution)/shard_map/ppermute | solution.py:184
  39.4 5.5 %collective-permute-done.1.refs_3_.q2 = bf16[384,1536]{1,0:T(8,128)(2,1)} collective-permute-done((bf16[384,1536]{1,0:T(8,128)(2,1)S(1)}, bf16[384,1536]{1,0:T(8,128)(2,1)}, u32[]{:S(2)}, u32[]{:S(2)}) %collective-permute-start.1) | collective-permute-done | bytes 1179680 | tf_op jit(solution)/shard_map/ppermute | solution.py:184
  45.0 19.0 %collective-permute-done.2.refs_4_.g1 = bf16[384,1536]{1,0:T(8,128)(2,1)} collective-permute-done((bf16[384,1536]{1,0:T(8,128)(2,1)}, bf16[384,1536]{1,0:T(8,128)(2,1)}, u32[]{:S(2)}, u32[]{:S(2)}) %collective-permute-start.2) | collective-permute-done | bytes 1179680 | tf_op jit(solution)/shard_map/ppermute | solution.py:184
  64.0 5.2 %collective-permute-done.3.refs_5_.g2 = bf16[384,1536]{1,0:T(8,128)(2,1)} collective-permute-done((bf16[384,1536]{1,0:T(8,128)(2,1)}, bf16[384,1536]{1,0:T(8,128)(2,1)}, u32[]{:S(2)}, u32[]{:S(2)}) %collective-permute-start.3) | collective-permute-done | bytes 1179680 | tf_op jit(solution)/shard_map/ppermute | solution.py:184
  69.2 12.0 %stats2.1 = (f32[12,4,384]{2,1,0:T(4,128)}, f32[12,4,384]{2,1,0:T(4,128)}) custom-call(bf16[384,1536]{1,0:T(8,128)(2,1)} %fusion.19.refs_0_.key_ref, bf16[384,1536]{1,0:T(8,128)(2,1)} %bitcast.60, bf16[384,1536]{1,0:T(8,128)(2,1)} %collective-permute-done.refs_2_.q1, bf16[384,1536]{1,0:T(8,128)(2,1)} %collective-permute-done.1.refs_3_.q2, ...), custom_call_target="tpu_custom_call" | custom-call | flops 1811939328 | bytes 7077888 | tf_op jit(solution)/shard_map/stats2/pallas_call | solution.py:57
  81.2 2.5 collective-permute-start.4
  83.7 1.3 collective-permute-start.5
  85.0 10.1 %stats1.1.own = f32[12,4,384]{2,1,0:T(4,128)} custom-call(bf16[384,1536]{1,0:T(8,128)(2,1)} %fusion.19.refs_0_.key_ref, bf16[384,1536]{1,0:T(8,128)(2,1)} %bitcast.61, bf16[384,1536]{1,0:T(8,128)(2,1)} %copy-done, bf16[384,1536]{1,0:T(8,128)(2,1)} %bitcast.3.refs_3_.g0), custom_call_target="tpu_custom_call" | custom-call | flops 905969664 | bytes 4718592 | tf_op jit(solution)/shard_map/stats1/pallas_call | solution.py:57
  95.1 0.6 copy-done.19
  95.7 0.6 copy-done.20
  96.3 1.7 combine.1
  98.1 4.5 %collective-permute-start.6 = (f32[12,4,384]{2,1,0:T(4,128)}, f32[12,4,384]{2,1,0:T(4,128)S(1)}, u32[]{:S(2)}, u32[]{:S(2)}) collective-permute-start(f32[12,4,384]{2,1,0:T(4,128)} %get-tuple-element.28), channel_id=1, source_target_pairs={{0,2},{2,4},{4,6},{1,3},{3,5},{5,7},{8,10},{10,12},{12,14},{9,11},... | collective-permute-start | bytes 221192 | tf_op jit(solution)/shard_map/ppermute | solution.py:184
  102.6 1.3 collective-permute-start.7
  103.9 1.0 collective-permute-done.6.c1
  104.9 4.2 %collective-permute-done.7.c2 = f32[12,4,384]{2,1,0:T(4,128)S(1)} collective-permute-done((f32[12,4,384]{2,1,0:T(4,128)}, f32[12,4,384]{2,1,0:T(4,128)S(1)}, u32[]{:S(2)}, u32[]{:S(2)}) %collective-permute-start.7) | collective-permute-done | bytes 73760 | tf_op jit(solution)/shard_map/ppermute | solution.py:184
  109.1 0.6 copy-done.13
  109.7 8.3 %grads.5 = (f32[384,512]{1,0:T(8,128)}, bf16[384,512]{1,0:T(8,128)(2,1)}, f32[384,512]{1,0:T(8,128)}, bf16[384,512]{1,0:T(8,128)(2,1)}, bf16[384,512]{1,0:T(8,128)(2,1)}) custom-call(bf16[384,1536]{1,0:T(8,128)(2,1)} %fusion.19.refs_0_.key_ref, bf16[384,1536]{1,0:T(8,128)(2,1)} %bitcast.62, bf16[384,1536]{1,0:T(8,128)(2,1)} %copy-done, ...), custom_call_target="tpu_custom_call" | custom-call | flops 2264924160 | bytes 5898240 | tf_op jit(solution)/shard_map/grads/pallas_call | solution.py:142
  118.0 1.3 collective-permute-start.13
  119.3 5.3 %collective-permute-start.12 = (bf16[384,512]{1,0:T(8,128)(2,1)}, bf16[384,512]{1,0:T(8,128)(2,1)}, u32[]{:S(2)}, u32[]{:S(2)}) collective-permute-start(bf16[384,512]{1,0:T(8,128)(2,1)} %get-tuple-element.37), channel_id=1, source_target_pairs={{0,2},{2,4},{4,6},{1,3},{3,5},{5,7},{8,10},{10,12},{12,14},{9,11},... | collective-permute-start | bytes 1179656 | tf_op jit(solution)/shard_map/ppermute | solution.py:184
  124.6 8.4 %grads.4 = (f32[384,512]{1,0:T(8,128)}, bf16[384,512]{1,0:T(8,128)(2,1)}, f32[384,512]{1,0:T(8,128)}, bf16[384,512]{1,0:T(8,128)(2,1)}, bf16[384,512]{1,0:T(8,128)(2,1)}) custom-call(bf16[384,1536]{1,0:T(8,128)(2,1)} %fusion.19.refs_0_.key_ref, bf16[384,1536]{1,0:T(8,128)(2,1)} %bitcast.63, bf16[384,1536]{1,0:T(8,128)(2,1)} %copy-done, ...), custom_call_target="tpu_custom_call" | custom-call | flops 2264924160 | bytes 5898240 | tf_op jit(solution)/shard_map/grads/pallas_call | solution.py:142
  133.0 1.3 collective-permute-start.11
  134.3 5.3 %collective-permute-start.10 = (bf16[384,512]{1,0:T(8,128)(2,1)}, bf16[384,512]{1,0:T(8,128)(2,1)}, u32[]{:S(2)}, u32[]{:S(2)}) collective-permute-start(bf16[384,512]{1,0:T(8,128)(2,1)} %get-tuple-element.34), channel_id=1, source_target_pairs={{0,2},{2,4},{4,6},{1,3},{3,5},{5,7},{8,10},{10,12},{12,14},{9,11},... | collective-permute-start | bytes 1179656 | tf_op jit(solution)/shard_map/ppermute | solution.py:184
  139.6 8.4 %grads.3 = (f32[384,512]{1,0:T(8,128)}, bf16[384,512]{1,0:T(8,128)(2,1)}, f32[384,512]{1,0:T(8,128)}, bf16[384,512]{1,0:T(8,128)(2,1)}, bf16[384,512]{1,0:T(8,128)(2,1)}) custom-call(bf16[384,1536]{1,0:T(8,128)(2,1)} %fusion.19.refs_0_.key_ref, bf16[384,1536]{1,0:T(8,128)(2,1)} %bitcast.64, bf16[384,1536]{1,0:T(8,128)(2,1)} %copy-done, ...), custom_call_target="tpu_custom_call" | custom-call | flops 2264924160 | bytes 5898240 | tf_op jit(solution)/shard_map/grads/pallas_call | solution.py:142
  148.0 1.4 collective-permute-start.9
  149.4 1.2 constant_dynamic-update-slice_fusion.2
  150.6 1.2 constant_dynamic-update-slice_fusion.1
  152.0 1.3 fusion.23
  153.2 1.1 maximum_bitcast_fusion
  154.3 4.6 %collective-permute-start.8 = (bf16[384,512]{1,0:T(8,128)(2,1)S(1)}, bf16[384,512]{1,0:T(8,128)(2,1)S(1)}, u32[]{:S(2)}, u32[]{:S(2)}) collective-permute-start(bf16[384,512]{1,0:T(8,128)(2,1)S(1)} %copy-done.31), channel_id=1, source_target_pairs={{0,2},{2,4},{4,6},{1,3},{3,5},{5,7},{8,10},{10,12},{12,14},{9,11},... | collective-permute-start | bytes 1179656 | tf_op jit(solution)/shard_map/ppermute | solution.py:184
  158.9 1.2 convert_add_fusion
  160.2 1.3 convert_add_fusion.1
  161.5 2.7 %collective-permute-done.8 = bf16[384,512]{1,0:T(8,128)(2,1)S(1)} collective-permute-done((bf16[384,512]{1,0:T(8,128)(2,1)S(1)}, bf16[384,512]{1,0:T(8,128)(2,1)S(1)}, u32[]{:S(2)}, u32[]{:S(2)}) %collective-permute-start.8) | collective-permute-done | bytes 393248 | tf_op jit(solution)/shard_map/ppermute | solution.py:184
  164.4 0.7 fusion.14
  165.2 2.4 all-reduce.1
  167.7 76.1 %all-reduce = (f32[1536]{0:T(1024)S(1)}, f32[1536]{0:T(1024)S(1)}) all-reduce(f32[1536]{0:T(1024)S(1)} %get-tuple-element.47, f32[1536]{0:T(1024)S(1)} %copy-done.21), channel_id=1, replica_groups=mesh['batch'=4,'tm'=4,'tensor'=2] {'batch','tm'}, use_global_device_ids=true, to_apply=%region_11.0 | all-reduce | flops 3072 | bytes 24576 | tf_op jit(solution)/shard_map/psum | solution.py:240
  244.4 3.0 %fusion.16 = bf16[1,384,1536]{2,1,0:T(8,128)(2,1)} fusion(bf16[1,384,1536]{2,1,0:T(8,128)(2,1)S(1)} %copy-done.1, f32[1,384,512]{2,1,0:T(8,128)S(1)} %bitcast.65, f32[1,384,512]{2,1,0:T(8,128)} %bitcast.66, f32[1,384,512]{2,1,0:T(8,128)} %bitcast.67, f32[384]{0:T(512)S(1)} %get-tuple-element.57, f32[1536]{0:T(1024)S(1)} %copy-done.17, f32[384]{0:T(512)S(1)} %copy-done.23), kind=kLoop, calls=%fused_computation.20 | loop fusion | flops 4718592 | bytes 4727808 | tf_op jit(solution)/shard_map/convert_element_type | solution.py:166
  247.5 1.5 fusion.25
  (74 shorter events, 2.2 us)
Async XLA Ops:
  0.6 25.6 %copy-start.2 = (bf16[1,384,1536]{2,1,0:T(8,128)(2,1)S(1)}, bf16[1,384,1536]{2,1,0:T(8,128)(2,1)}, u32[]{:S(2)}) copy-start(bf16[1,384,1536]{2,1,0:T(8,128)(2,1)} %param.8) | copy-start | bytes 3538948
  0.6 7.1 %copy-start.1 = (bf16[1,384,1536]{2,1,0:T(8,128)(2,1)S(1)}, bf16[1,384,1536]{2,1,0:T(8,128)(2,1)}, u32[]{:S(2)}) copy-start(bf16[1,384,1536]{2,1,0:T(8,128)(2,1)} %param.7) | copy-start | bytes 3538948
  0.7 7.1 %copy-start.17 = (f32[1536]{0:T(1024)S(1)}, f32[1536]{0:T(1024)}, u32[]{:S(2)}) copy-start(f32[1536]{0:T(1024)} %param.11) | copy-start | bytes 18436
  0.7 25.5 %copy-start.18 = (f32[1536]{0:T(1024)S(1)}, f32[1536]{0:T(1024)}, u32[]{:S(2)}) copy-start(f32[1536]{0:T(1024)} %param.12) | copy-start | bytes 18436
  7.2 0.5 copy-start.29
  7.7 0.6 copy-start.22
  8.3 72.9 %copy-start = (bf16[384,1536]{1,0:T(8,128)(2,1)}, bf16[384,1536]{1,0:T(8,128)(2,1)S(1)}, u32[]{:S(2)}) copy-start(bf16[384,1536]{1,0:T(8,128)(2,1)S(1)} %fusion.10.refs_2_.q0) | copy-start | bytes 3538948
  8.3 31.1 %collective-permute-start = (bf16[384,1536]{1,0:T(8,128)(2,1)S(1)}, bf16[384,1536]{1,0:T(8,128)(2,1)}, u32[]{:S(2)}, u32[]{:S(2)}) collective-permute-start(bf16[384,1536]{1,0:T(8,128)(2,1)S(1)} %fusion.10.refs_2_.q0), channel_id=1, source_target_pairs={{0,2},{2,4},{4,6},{1,3},{3,5},{5,7},{8,10},{10,12},{12,14},{9,11},... | collective-permute-start | bytes 3538952 | tf_op jit(solution)/shard_map/ppermute | solution.py:184
  14.2 30.8 %collective-permute-start.1 = (bf16[384,1536]{1,0:T(8,128)(2,1)S(1)}, bf16[384,1536]{1,0:T(8,128)(2,1)}, u32[]{:S(2)}, u32[]{:S(2)}) collective-permute-start(bf16[384,1536]{1,0:T(8,128)(2,1)S(1)} %fusion.10.refs_2_.q0), channel_id=1, source_target_pairs={{2,0},{4,2},{6,4},{3,1},{5,3},{7,5},{10,8},{12,10},{14,12},{11,9},... | collective-permute-start | bytes 3538952 | tf_op jit(solution)/shard_map/ppermute | solution.py:184
  15.4 48.6 %collective-permute-start.2 = (bf16[384,1536]{1,0:T(8,128)(2,1)}, bf16[384,1536]{1,0:T(8,128)(2,1)}, u32[]{:S(2)}, u32[]{:S(2)}) collective-permute-start(bf16[384,1536]{1,0:T(8,128)(2,1)} %bitcast.3.refs_3_.g0), channel_id=1, source_target_pairs={{0,2},{2,4},{4,6},{1,3},{3,5},{5,7},{8,10},{10,12},{12,14},{9,11},... | collective-permute-start | bytes 3538952 | tf_op jit(solution)/shard_map/ppermute | solution.py:184
  21.0 48.2 %collective-permute-start.3 = (bf16[384,1536]{1,0:T(8,128)(2,1)}, bf16[384,1536]{1,0:T(8,128)(2,1)}, u32[]{:S(2)}, u32[]{:S(2)}) collective-permute-start(bf16[384,1536]{1,0:T(8,128)(2,1)} %bitcast.3.refs_3_.g0), channel_id=1, source_target_pairs={{2,0},{4,2},{6,4},{3,1},{5,3},{7,5},{10,8},{12,10},{14,12},{11,9},... | collective-permute-start | bytes 3538952 | tf_op jit(solution)/shard_map/ppermute | solution.py:184
  26.2 18.8 %copy-start.24 = (f32[384]{0:T(512)}, f32[384]{0:T(512)S(1)}, u32[]{:S(2)}) copy-start(f32[384]{0:T(512)S(1)} %add_rsqrt_fusion) | copy-start | bytes 4612
  81.2 13.9 %collective-permute-start.4 = (f32[12,4,384]{2,1,0:T(4,128)}, f32[12,4,384]{2,1,0:T(4,128)S(1)}, u32[]{:S(2)}, u32[]{:S(2)}) collective-permute-start(f32[12,4,384]{2,1,0:T(4,128)} %get-tuple-element.25), channel_id=1, source_target_pairs={{0,2},{2,4},{4,6},{1,3},{3,5},{5,7},{8,10},{10,12},{12,14},{9,11},... | collective-permute-start | bytes 221192 | tf_op jit(solution)/shard_map/ppermute | solution.py:184
  83.7 11.4 %collective-permute-start.5 = (f32[12,4,384]{2,1,0:T(4,128)}, f32[12,4,384]{2,1,0:T(4,128)S(1)}, u32[]{:S(2)}, u32[]{:S(2)}) collective-permute-start(f32[12,4,384]{2,1,0:T(4,128)} %get-tuple-element.26), channel_id=1, source_target_pairs={{2,0},{4,2},{6,4},{3,1},{5,3},{7,5},{10,8},{12,10},{14,12},{11,9},... | collective-permute-start | bytes 221192 | tf_op jit(solution)/shard_map/ppermute | solution.py:184
  95.1 0.6 copy-start.19
  95.7 0.6 copy-start.20
  98.1 6.8 %collective-permute-start.6 = (f32[12,4,384]{2,1,0:T(4,128)}, f32[12,4,384]{2,1,0:T(4,128)S(1)}, u32[]{:S(2)}, u32[]{:S(2)}) collective-permute-start(f32[12,4,384]{2,1,0:T(4,128)} %get-tuple-element.28), channel_id=1, source_target_pairs={{0,2},{2,4},{4,6},{1,3},{3,5},{5,7},{8,10},{10,12},{12,14},{9,11},... | collective-permute-start | bytes 221192 | tf_op jit(solution)/shard_map/ppermute | solution.py:184
  102.6 6.5 %collective-permute-start.7 = (f32[12,4,384]{2,1,0:T(4,128)}, f32[12,4,384]{2,1,0:T(4,128)S(1)}, u32[]{:S(2)}, u32[]{:S(2)}) collective-permute-start(f32[12,4,384]{2,1,0:T(4,128)} %get-tuple-element.29), channel_id=1, source_target_pairs={{2,0},{4,2},{6,4},{3,1},{5,3},{7,5},{10,8},{12,10},{14,12},{11,9},... | collective-permute-start | bytes 221192 | tf_op jit(solution)/shard_map/ppermute | solution.py:184
  104.9 4.2 %copy-start.12 = (f32[12,4,384]{2,1,0:T(4,128)}, f32[12,4,384]{2,1,0:T(4,128)S(1)}, u32[]{:S(2)}) copy-start(f32[12,4,384]{2,1,0:T(4,128)S(1)} %collective-permute-done.6.c1) | copy-start | bytes 221188
  109.1 0.6 copy-start.13
  118.0 36.3 %collective-permute-start.13 = (bf16[384,512]{1,0:T(8,128)(2,1)}, bf16[384,512]{1,0:T(8,128)(2,1)S(1)}, u32[]{:S(2)}, u32[]{:S(2)}) collective-permute-start(bf16[384,512]{1,0:T(8,128)(2,1)} %get-tuple-element.38), channel_id=1, source_target_pairs={{2,0},{4,2},{6,4},{3,1},{5,3},{7,5},{10,8},{12,10},{14,12},{11,9},... | collective-permute-start | bytes 1179656 | tf_op jit(solution)/shard_map/ppermute | solution.py:184
  119.3 39.6 %collective-permute-start.12 = (bf16[384,512]{1,0:T(8,128)(2,1)}, bf16[384,512]{1,0:T(8,128)(2,1)}, u32[]{:S(2)}, u32[]{:S(2)}) collective-permute-start(bf16[384,512]{1,0:T(8,128)(2,1)} %get-tuple-element.37), channel_id=1, source_target_pairs={{0,2},{2,4},{4,6},{1,3},{3,5},{5,7},{8,10},{10,12},{12,14},{9,11},... | collective-permute-start | bytes 1179656 | tf_op jit(solution)/shard_map/ppermute | solution.py:184
  133.0 27.1 %collective-permute-start.11 = (bf16[384,512]{1,0:T(8,128)(2,1)}, bf16[384,512]{1,0:T(8,128)(2,1)}, u32[]{:S(2)}, u32[]{:S(2)}) collective-permute-start(bf16[384,512]{1,0:T(8,128)(2,1)} %get-tuple-element.35), channel_id=1, source_target_pairs={{2,0},{4,2},{6,4},{3,1},{5,3},{7,5},{10,8},{12,10},{14,12},{11,9},... | collective-permute-start | bytes 1179656 | tf_op jit(solution)/shard_map/ppermute | solution.py:184
  134.3 25.9 %collective-permute-start.10 = (bf16[384,512]{1,0:T(8,128)(2,1)}, bf16[384,512]{1,0:T(8,128)(2,1)}, u32[]{:S(2)}, u32[]{:S(2)}) collective-permute-start(bf16[384,512]{1,0:T(8,128)(2,1)} %get-tuple-element.34), channel_id=1, source_target_pairs={{0,2},{2,4},{4,6},{1,3},{3,5},{5,7},{8,10},{10,12},{12,14},{9,11},... | collective-permute-start | bytes 1179656 | tf_op jit(solution)/shard_map/ppermute | solution.py:184
  148.0 3.8 %copy-start.5 = (f32[384,512]{1,0:T(8,128)S(1)}, f32[384,512]{1,0:T(8,128)}, u32[]{:S(2)}) copy-start(f32[384,512]{1,0:T(8,128)} %get-tuple-element.41) | copy-start | bytes 2359300
  148.0 13.5 %collective-permute-start.9 = (bf16[384,512]{1,0:T(8,128)(2,1)}, bf16[384,512]{1,0:T(8,128)(2,1)S(1)}, u32[]{:S(2)}, u32[]{:S(2)}) collective-permute-start(bf16[384,512]{1,0:T(8,128)(2,1)} %get-tuple-element.32), channel_id=1, source_target_pairs={{2,0},{4,2},{6,4},{3,1},{5,3},{7,5},{10,8},{12,10},{14,12},{11,9},... | collective-permute-start | bytes 1179656 | tf_op jit(solution)/shard_map/ppermute | solution.py:184
  149.4 2.5 %copy-start.25 = (f32[384]{0:T(512)S(1)}, f32[384]{0:T(512)}, u32[]{:S(2)}) copy-start(f32[384]{0:T(512)} %copy-done.24) | copy-start | bytes 4612
  151.8 1.4 copy-start.14
  151.8 1.4 copy-start.15
  151.9 1.4 copy-start.16
  151.9 2.4 copy-start.31
  151.9 7.0 %copy-start.9 = (f32[384,512]{1,0:T(8,128)S(1)}, f32[384,512]{1,0:T(8,128)}, u32[]{:S(2)}) copy-start(f32[384,512]{1,0:T(8,128)} %get-tuple-element.36) | copy-start | bytes 2359300
  153.2 6.9 %copy-start.10 = (f32[384,512]{1,0:T(8,128)S(1)}, f32[384,512]{1,0:T(8,128)}, u32[]{:S(2)}) copy-start(f32[384,512]{1,0:T(8,128)} %get-tuple-element.33) | copy-start | bytes 2359300
  154.3 9.8 %collective-permute-start.8 = (bf16[384,512]{1,0:T(8,128)(2,1)S(1)}, bf16[384,512]{1,0:T(8,128)(2,1)S(1)}, u32[]{:S(2)}, u32[]{:S(2)}) collective-permute-start(bf16[384,512]{1,0:T(8,128)(2,1)S(1)} %copy-done.31), channel_id=1, source_target_pairs={{0,2},{2,4},{4,6},{1,3},{3,5},{5,7},{8,10},{10,12},{12,14},{9,11},... | collective-permute-start | bytes 1179656 | tf_op jit(solution)/shard_map/ppermute | solution.py:184
  158.9 5.2 %copy-start.11 = (f32[384,512]{1,0:T(8,128)S(1)}, f32[384,512]{1,0:T(8,128)}, u32[]{:S(2)}) copy-start(f32[384,512]{1,0:T(8,128)} %get-tuple-element.30) | copy-start | bytes 2359300
  160.2 4.1 %copy-start.23 = (f32[384]{0:T(512)S(1)}, f32[384]{0:T(512)}, u32[]{:S(2)}) copy-start(f32[384]{0:T(512)} %copy-done.22) | copy-start | bytes 4612
  161.5 3.6 %copy-start.3 = (f32[384,512]{1,0:T(8,128)}, f32[384,512]{1,0:T(8,128)S(1)}, u32[]{:S(2)}) copy-start(f32[384,512]{1,0:T(8,128)S(1)} %convert_add_fusion.1) | copy-start | bytes 2359300
  164.3 0.9 copy-start.4
  164.3 0.9 copy-start.27
  164.4 3.3 %copy-start.28 = (f32[384]{0:T(512)S(1)}, f32[384]{0:T(512)}, u32[]{:S(2)}) copy-start(f32[384]{0:T(512)} %get-tuple-element.55) | copy-start | bytes 4612
  164.4 3.3 %copy-start.30 = (f32[384]{0:T(512)S(1)}, f32[384]{0:T(512)}, u32[]{:S(2)}) copy-start(f32[384]{0:T(512)} %copy-done.29) | copy-start | bytes 4612
  164.4 3.3 %copy-start.21 = (f32[1536]{0:T(1024)S(1)}, f32[1536]{0:T(1024)}, u32[]{:S(2)}) copy-start(f32[1536]{0:T(1024)} %get-tuple-element.45) | copy-start | bytes 18436
  244.4 3.1 %copy-start.6 = (f32[384,512]{1,0:T(8,128)S(1)}, f32[384,512]{1,0:T(8,128)}, u32[]{:S(2)}) copy-start(f32[384,512]{1,0:T(8,128)} %get-tuple-element.41) | copy-start | bytes 2359300
  244.4 3.1 %copy-start.7 = (f32[384,512]{1,0:T(8,128)S(1)}, f32[384,512]{1,0:T(8,128)}, u32[]{:S(2)}) copy-start(f32[384,512]{1,0:T(8,128)} %get-tuple-element.40) | copy-start | bytes 2359300
  244.4 3.1 %copy-start.8 = (f32[384,512]{1,0:T(8,128)S(1)}, f32[384,512]{1,0:T(8,128)}, u32[]{:S(2)}) copy-start(f32[384,512]{1,0:T(8,128)} %get-tuple-element.39) | copy-start | bytes 2359300
  244.4 3.1 %copy-start.26 = (f32[384]{0:T(512)S(1)}, f32[384]{0:T(512)}, u32[]{:S(2)}) copy-start(f32[384]{0:T(512)} %copy-done.24) | copy-start | bytes 4612

commit v2 on v0

v2 whole, which is shorter than its diff:
```python
import math

import jax
import jax.numpy as jnp
from jax import lax
from jax.experimental import pallas as pl
from jax.experimental.pallas import tpu as pltpu
from jax.sharding import PartitionSpec as P

HD = 128
STATS = 4
EPSILON = 1e-06
DEAD = 1e30
SCALE = HD ** (-0.5)
GROUP = 2
MESH = pl.DeviceIdType.MESH


def cols_dot(left, right):
    return lax.dot_general(
        left, right, (((1,), (1,)), ((), ())), preferred_element_type=jnp.float32
    )


def rows_dot(left, right):
    return lax.dot_general(
        left, right, (((0,), (0,)), ((), ())), preferred_element_type=jnp.float32
    )


def tile_stats(key, value, query, grad):
    scores = cols_dot(key, query) * SCALE
    highest = jnp.max(scores, axis=0, keepdims=True)
    exponent = jnp.exp(scores - highest)
    dprobs = cols_dot(value, grad)
    total = jnp.sum(exponent, axis=0, keepdims=True)
    weighted = jnp.sum(exponent * dprobs, axis=0, keepdims=True)
    return highest, total, weighted


def attention_body(group, chunks, live, q, k, v, g, dq, dk, dv,
                   rq, rg, st_own, st_out, st_in, co_own, co_out, co_in, dq_out, dq_in,
                   bulk_send, bulk_recv, st_send, st_recv, co_send, co_recv, dq_send, dq_recv):
    rows = q.shape[0]
    span = group * HD
    me = lax.axis_index("tm")
    peers = lax.axis_size("tm")
    has = (me > 0, me < peers - 1)
    target = (jnp.maximum(me - 1, 0), jnp.minimum(me + 1, peers - 1))

    def part(chunk):
        return pl.ds(pl.multiple_of(chunk * span, HD), span)

    def remote(source, sink, send, recv, side):
        return pltpu.make_async_remote_copy(
            src_ref=source, dst_ref=sink, send_sem=send, recv_sem=recv,
            device_id={"tm": target[side]}, device_id_type=MESH,
        )

    def bulk(chunk, side, slot):
        where = part(chunk)
        return (
            remote(g.at[:, where], rg.at[slot, :, where],
                   bulk_send.at[side, 0, chunk], bulk_recv.at[slot, 0, chunk], side),
            remote(q.at[:, where], rq.at[slot, :, where],
                   bulk_send.at[side, 1, chunk], bulk_recv.at[slot, 1, chunk], side),
        )

    def small(out, into, send, recv, chunk, side, slot):
        where = pl.ds(chunk * group, group)
        return remote(out.at[side, where], into.at[slot, where],
                      send.at[side, chunk], recv.at[slot, chunk], side)

    def stat_copy(chunk, side, slot):
        return small(st_out, st_in, st_send, st_recv, chunk, side, slot)

    def comb_copy(chunk, side, slot):
        return small(co_out, co_in, co_send, co_recv, chunk, side, slot)

    def dq_copy(chunk, side, slot):
        where = part(chunk)
        return remote(dq_out.at[side, :, where], dq_in.at[slot, :, where],
                      dq_send.at[side, chunk], dq_recv.at[slot, chunk], side)

    barrier = pltpu.get_barrier_semaphore()
    for side in range(2):
        @pl.when(has[side])
        def _():
            pl.semaphore_signal(barrier, inc=1, device_id={"tm": target[side]}, device_id_type=MESH)
    pl.semaphore_wait(barrier, (me > 0).astype(jnp.int32) + (me < peers - 1).astype(jnp.int32))

    def start_bulk(chunk):
        for side in range(2):
            @pl.when(has[side])
            def _():
                for copy in bulk(chunk, side, 1 - side):
                    copy.start()

    for chunk in range(min(2, chunks)):
        start_bulk(chunk)
    for side in range(2):
        @pl.when(jnp.logical_not(has[side]))
        def _():
            rq[side] = jnp.zeros(rq.shape[1:], rq.dtype)
            rg[side] = jnp.zeros(rg.shape[1:], rg.dtype)
            dq_in[side] = jnp.zeros(dq_in.shape[1:], dq_in.dtype)
            st_in[side] = jnp.zeros(st_in.shape[1:], st_in.dtype)
            co_in[side] = jnp.zeros(co_in.shape[1:], co_in.dtype)

    def column(head):
        return pl.ds(pl.multiple_of(head * HD, HD), HD)

    def put_stats(ref, index, values):
        for row, value in enumerate(values):
            ref[index + (slice(row, row + 1), slice(None))] = value

    def step(s, carry):
        @pl.when(s < chunks)
        def _():
            for side in range(2):
                @pl.when(has[side])
                def _():
                    for copy in bulk(s, side, side):
                        copy.wait_recv()
            for inner in range(group):
                head = s * group + inner
                col = column(head)
                for side in range(2):
                    put_stats(st_out, (side, head), tile_stats(
                        k[:, col], v[:, col], rq[side, :, col], rg[side, :, col]))

        @pl.when((s >= 1) & (s <= chunks))
        def _():
            for side in range(2):
                @pl.when(has[side])
                def _():
                    stat_copy(s - 1, side, side).wait_recv()
            where = pl.ds((s - 1) * group, group)
            alive = (live[0:1, :] > 0.5, live[1:2, :] > 0.5)
            highest = st_own[where, 0:1, :]
            for side in range(2):
                highest = jnp.where(
                    alive[side], jnp.maximum(highest, st_in[side, where, 0:1, :]), highest)
            weight = jnp.exp(st_own[where, 0:1, :] - highest)
            total = weight * st_own[where, 1:2, :]
            delta = weight * st_own[where, 2:3, :]
            for side in range(2):
                weight = jnp.exp(jnp.minimum(st_in[side, where, 0:1, :] - highest, 0.0))
                total = total + jnp.where(alive[side], weight * st_in[side, where, 1:2, :], 0.0)
                delta = delta + jnp.where(alive[side], weight * st_in[side, where, 2:3, :], 0.0)
            inverse = 1.0 / total
            delta = delta * inverse
            co_own[where, 0:1, :] = highest
            co_own[where, 1:2, :] = inverse
            co_own[where, 2:3, :] = delta
            for side in range(2):
                co_out[side, where, 0:1, :] = jnp.where(alive[side], highest, DEAD)
                co_out[side, where, 1:2, :] = inverse
                co_out[side, where, 2:3, :] = delta

        @pl.when(s < chunks)
        def _():
            for side in range(2):
                @pl.when(has[side])
                def _():
                    stat_copy(s, side, 1 - side).start()

            @pl.when(s + 2 < chunks)
            def _():
                start_bulk(s + 2)
            for inner in range(group):
                head = s * group + inner
                col = column(head)
                put_stats(st_own, (head,), tile_stats(k[:, col], v[:, col], q[:, col], g[:, col]))

        @pl.when((s >= 1) & (s <= chunks))
        def _():
            for side in range(2):
                @pl.when(has[side])
                def _():
                    comb_copy(s - 1, side, 1 - side).start()

        @pl.when(s >= 2)
        def _():
            chunk = s - 2
            for side in range(2):
                @pl.when(has[side])
                def _():
                    comb_copy(chunk, side, side).wait_recv()
            for inner in range(group):
                head = chunk * group + inner
                col = column(head)
                key = k[:, col]
                value = v[:, col]
                key_total = None
                value_total = None
                for t in range(3):
                    if t < 2:
                        query, grad, stat = rq[t, :, col], rg[t, :, col], co_in.at[t]
                    else:
                        query, grad, stat = q[:, col], g[:, col], co_own
                    scores = cols_dot(key, query) * SCALE
                    probs = jnp.exp(scores - stat[head, 0:1, :]) * stat[head, 1:2, :]
                    dprobs = cols_dot(value, grad)
                    dscore = (probs * (dprobs - stat[head, 2:3, :])).astype(jnp.bfloat16)
                    probs_b = probs.astype(jnp.bfloat16)
                    value_term = jnp.dot(probs_b, grad, preferred_element_type=jnp.float32)
                    key_term = jnp.dot(dscore, query, preferred_element_type=jnp.float32)
                    value_total = value_term if t == 0 else value_total + value_term
                    key_total = key_term if t == 0 else key_total + key_term
                    result = rows_dot(key, dscore).T * SCALE
                    if t < 2:
                        dq_out[t, :, col] = result.astype(dq_out.dtype)
                    else:
                        dq[:, col] = result
                dk[:, col] = key_total * SCALE
                dv[:, col] = value_total.astype(dv.dtype)
            for side in range(2):
                @pl.when(has[side])
                def _():
                    dq_copy(chunk, side, 1 - side).start()
        return carry

    lax.fori_loop(0, chunks + 2, step, 0)

    def drain(chunk, carry):
        for side in range(2):
            @pl.when(has[side])
            def _():
                dq_copy(chunk, side, side).wait_recv()
        where = part(chunk)
        dq[:, where] = (
            dq[:, where]
            + dq_in[0, :, where].astype(jnp.float32)
            + dq_in[1, :, where].astype(jnp.float32)
        )
        for side in range(2):
            @pl.when(has[side])
            def _():
                for copy in bulk(chunk, side, 1 - side):
                    copy.wait_send()
                stat_copy(chunk, side, 1 - side).wait_send()
                comb_copy(chunk, side, 1 - side).wait_send()
                dq_copy(chunk, side, 1 - side).wait_send()
        return carry

    lax.fori_loop(0, chunks, drain, 0)


def attention(live, query, key, value, grad):
    rows, width = query.shape
    heads = width // HD
    group = math.gcd(GROUP, heads)
    chunks = heads // group
    whole = pl.BlockSpec(memory_space=pltpu.VMEM)
    stat = (heads, STATS, rows)
    dma = pltpu.SemaphoreType.DMA

    def body(*refs):
        attention_body(group, chunks, *refs)

    return pl.pallas_call(
        body,
        out_shape=[
            jax.ShapeDtypeStruct((rows, width), jnp.float32),
            jax.ShapeDtypeStruct((rows, width), jnp.float32),
            jax.ShapeDtypeStruct((rows, width), jnp.bfloat16),
        ],
        in_specs=[whole] * 5,
        out_specs=[whole] * 3,
        scratch_shapes=[
            pltpu.VMEM((2, rows, width), jnp.bfloat16),
            pltpu.VMEM((2, rows, width), jnp.bfloat16),
            pltpu.VMEM(stat, jnp.float32),
            pltpu.VMEM((2,) + stat, jnp.float32),
            pltpu.VMEM((2,) + stat, jnp.float32),
            pltpu.VMEM(stat, jnp.float32),
            pltpu.VMEM((2,) + stat, jnp.float32),
            pltpu.VMEM((2,) + stat, jnp.float32),
            pltpu.VMEM((2, rows, width), jnp.bfloat16),
            pltpu.VMEM((2, rows, width), jnp.bfloat16),
            dma((2, 2, chunks)), dma((2, 2, chunks)),
            dma((2, chunks)), dma((2, chunks)),
            dma((2, chunks)), dma((2, chunks)),
            dma((2, chunks)), dma((2, chunks)),
        ],
        compiler_params=pltpu.CompilerParams(collective_id=0, has_side_effects=True),
        name="attention",
    )(live, query, key, value, grad)


def totals_body(gains, proj, gain_sum, proj_sum, gain_slots, proj_slots,
                gain_send, gain_recv, proj_send, proj_recv):
    tm = lax.axis_size("tm")
    count = lax.axis_size("batch") * tm
    me = lax.axis_index("batch") * tm + lax.axis_index("tm")
    cores = lax.axis_size("tensor")
    core = lax.axis_index("tensor")
    barrier = pltpu.get_barrier_semaphore()

    def gain_peer(i):
        return lax.rem(me + i, count)

    def gain_id(peer):
        return {"batch": lax.div(peer, tm), "tm": lax.rem(peer, tm)}

    def core_peer(i):
        return lax.rem(core + i, cores)

    def greet_gain(i, carry):
        pl.semaphore_signal(barrier, inc=1, device_id=gain_id(gain_peer(i)), device_id_type=MESH)
        return carry

    def greet_core(i, carry):
        pl.semaphore_signal(barrier, inc=1, device_id={"tensor": core_peer(i)}, device_id_type=MESH)
        return carry

    lax.fori_loop(1, count, greet_gain, 0)
    lax.fori_loop(1, cores, greet_core, 0)
    gain_slots[me] = gains[...]
    proj_slots[core] = proj[...]
    pl.semaphore_wait(barrier, count - 1 + cores - 1)

    def gain_copy(slot, peer):
        return pltpu.make_async_remote_copy(
            src_ref=gains, dst_ref=gain_slots.at[slot], send_sem=gain_send.at[peer],
            recv_sem=gain_recv.at[slot], device_id=gain_id(peer), device_id_type=MESH,
        )

    def proj_copy(slot, peer):
        return pltpu.make_async_remote_copy(
            src_ref=proj, dst_ref=proj_slots.at[slot], send_sem=proj_send.at[peer],
            recv_sem=proj_recv.at[slot], device_id={"tensor": peer}, device_id_type=MESH,
        )

    def send_core(i, carry):
        proj_copy(core, core_peer(i)).start()
        return carry

    def send_gain(i, carry):
        gain_copy(me, gain_peer(i)).start()
        return carry

    def end_core(i, carry):
        peer = core_peer(i)
        proj_copy(core, peer).wait_send()
        proj_copy(peer, peer).wait_recv()
        return carry

    def end_gain(i, carry):
        peer = gain_peer(i)
        gain_copy(me, peer).wait_send()
        gain_copy(peer, peer).wait_recv()
        return carry

    lax.fori_loop(1, cores, send_core, 0)
    lax.fori_loop(1, count, send_gain, 0)
    lax.fori_loop(1, cores, end_core, 0)
    lax.fori_loop(1, count, end_gain, 0)
    proj_sum[...] = jnp.sum(proj_slots[...], axis=0)
    gain_sum[...] = jnp.sum(gain_slots[...], axis=0)


def totals(gains, proj):
    count = lax.axis_size("batch") * lax.axis_size("tm")
    cores = lax.axis_size("tensor")
    whole = pl.BlockSpec(memory_space=pltpu.VMEM)
    dma = pltpu.SemaphoreType.DMA
    return pl.pallas_call(
        totals_body,
        out_shape=[
            jax.ShapeDtypeStruct(gains.shape, jnp.float32),
            jax.ShapeDtypeStruct(proj.shape, jnp.float32),
        ],
        in_specs=[whole] * 2,
        out_specs=[whole] * 2,
        scratch_shapes=[
            pltpu.VMEM((count,) + gains.shape, jnp.float32),
            pltpu.VMEM((cores,) + proj.shape, jnp.float32),
            dma((count,)), dma((count,)), dma((cores,)), dma((cores,)),
        ],
        compiler_params=pltpu.CompilerParams(collective_id=1, has_side_effects=True),
        name="totals",
    )(gains, proj)


def finish_norm(wide_rows, inverse, gain_row, grad_normed, projection, feature_count):
    cubed = inverse * inverse * inverse
    grad_rows = (
        inverse[:, None] * gain_row[None, :] * grad_normed
        - wide_rows * (cubed * projection / feature_count)[:, None]
    )
    return grad_rows.astype(jnp.bfloat16)


def shards(q_raw, k_raw, values, grad_out, gain_q, gain_k, tile_lists):
    query_wide = q_raw[0].astype(jnp.float32)
    key_wide = k_raw[0].astype(jnp.float32)
    value_rows = values[0]
    grad_rows = grad_out[0]
    entries = tile_lists[0, 0]
    token_count, feature_count = query_wide.shape
    width_all = feature_count * lax.axis_size("tensor")
    count_all = lax.axis_size("batch") * lax.axis_size("tm") * token_count
    squares = lax.psum(
        (jnp.sum(query_wide * query_wide, axis=1), jnp.sum(key_wide * key_wide, axis=1)), "tensor"
    )
    inverse_q = lax.rsqrt(squares[0] / width_all + EPSILON)
    inverse_k = lax.rsqrt(squares[1] / width_all + EPSILON)
    query_norm = (query_wide * inverse_q[:, None] * gain_q[None, :]).astype(jnp.bfloat16)
    key_norm = (key_wide * inverse_k[:, None] * gain_k[None, :]).astype(jnp.bfloat16)
    position = lax.axis_index("tm")
    live = jnp.stack(
        [
            jnp.any((entries >= 0) & (entries == position - 1)),
            jnp.any((entries >= 0) & (entries == position + 1)),
        ]
    ).astype(jnp.float32)
    live = jnp.broadcast_to(live[:, None], (2, token_count))
    grad_query, grad_kn, grad_values = attention(live, query_norm, key_norm, value_rows, grad_rows)
    gain_terms, proj = totals(
        jnp.stack(
            [
                jnp.sum(grad_query * query_wide * inverse_q[:, None], axis=0),
                jnp.sum(grad_kn * key_wide * inverse_k[:, None], axis=0),
            ]
        ),
        jnp.stack(
            [
                jnp.sum(query_wide * gain_q[None, :] * grad_query, axis=1),
                jnp.sum(key_wide * gain_k[None, :] * grad_kn, axis=1),
            ]
        ),
    )
    grad_q = finish_norm(query_wide, inverse_q, gain_q, grad_query, proj[0], width_all)
    grad_k = finish_norm(key_wide, inverse_k, gain_k, grad_kn, proj[1], width_all)
    factor_all = 1.0 / math.sqrt(count_all)
    return (
        grad_q[None],
        grad_k[None],
        grad_values[None],
        gain_terms[0] * factor_all,
        gain_terms[1] * factor_all,
    )


def solution(mesh):
    rows = P("batch", "tm", "tensor")
    return jax.shard_map(
        shards,
        mesh=mesh,
        in_specs=(rows, rows, rows, rows, P("tensor"), P("tensor"), P("batch", "tm", None)),
        out_specs=(rows, rows, rows, P("tensor"), P("tensor")),
        check_vma=False,
    )
```

time: 476 us -> 126 us (0.26)
  Pallas kernels: 0 us -> 101 us
  waiting for transfers between devices: 101 us -> 0 us
  matrix products: 95.5 us -> 0 us
  local copies, waits for them, and re-layouts: 95.2 us -> 2.49 us
  blocking collectives: 82.1 us -> 2.62 us
  other arithmetic: 77.5 us -> 18.6 us
  starting transfers between devices: 13.6 us -> 0 us
  loops' own time: 8.21 us -> 0 us
    pallas_call x0 -> x2, Pallas kernels: none -> 101 us  [the longest x1 90.7 us: attention(): pl.pallas_call(body, out_shape=[jax.ShapeDtypeStruct((rows, width), jnp.f...]
    ppermute x4 -> x0, waiting for transfers between devices: 101 us -> none  [the longest x2 52.3 us: padded(): after = lax.ppermute(first, axis, down)]
    dot_general x60 -> x0, matrix products: 95.5 us -> none  [the longest x24 55.1 us: contract_rows(): lax.dot_general(left_side, right_side, (((0,), (0,)), ((), ())), preferre...]
    psum x2 -> x0, blocking collectives: 79.4 us -> none  [the longest x1 77 us: shards(): lax.psum((jnp.sum(grad_query * query_wide * inverse_q[:, None], axis=0),...]
    another operation x2 -> x4, local copies, waits for them, and re-layouts: 22.3 us -> 0.02 us  [the longest x2 0.01 us: shards(): jnp.stack([jnp.sum(query_wide * gain_q[None, :] * grad_query, axis=1), jn...]
    convert_element_type x15 -> x1, other arithmetic: 22.6 us -> 1.37 us  [shards(): live = jnp.stack([jnp.any((entries >= 0) & (entries == position - 1)), jn...]
    dynamic_slice x24 -> x0, local copies, waits for them, and re-layouts: 20.2 us -> none  [the longest x12 13.3 us: head_slice(): return lax.dynamic_slice_in_dim(source, column, HD, source.ndim - 1)]
    scatter-add x1 -> x0, other arithmetic: 19.9 us -> none  [shards(): grad_buffer = grad_buffer.at[:, places].add(grad_pair)]
  transfers between devices with their start and end apart: 4 -> 0, of which waited for: 4 -> 0; matrix products, arithmetic and copies ran while one was open for 1% -> 0% of each run, Pallas kernels for 0% -> 0%
where the time goes in v2:
time: 126 us
  Pallas kernels  101 us (80%)
  other arithmetic  18.6 us (15%)
  blocking collectives  2.62 us (2%)
  local copies, waits for them, and re-layouts  2.49 us (2%)
    pallas_call x1, Pallas kernels, attention(): pl.pallas_call(body, out_shape=[jax.ShapeDtypeStruct((rows, width), jnp.f...  90.7 us
    pallas_call x1, Pallas kernels, totals(): pl.pallas_call(totals_body, out_shape=[jax.ShapeDtypeStruct(gains.shape,...  10.4 us
    broadcast_in_dim x1, other arithmetic, shards(): grad_k[None]  3.34 us
    psum x1, blocking collectives, shards(): lax.psum((jnp.sum(query_wide * query_wide, axis=1), jnp.sum(key_wide * ke...  2.62 us

profile of v2, /device:TPU:0, one launch (start us, length us, event | category | flops | bytes accessed | tf_op | source)
XLA Modules:
  0.0 125.5 jit_solution(16701322282745943042)
XLA Ops:
  0.6 0.0 copy-start
  0.6 0.0 copy-start.5
  0.7 1.4 %and_reduce_fusion.1 = (pred[]{:T(512)}, pred[]{:T(512)}) fusion(s32[1,1,3]{2,1,0:T(1,128)} %param.13, s32[]{:T(128)S(6)} %sub.9, s32[]{:T(128)S(6)} %add.15), kind=kLoop, calls=%fused_computation.44 | loop fusion | flops 19 | bytes 22 | tf_op jit(solution)/shard_map/reduce_or | solution.py:415
  2.1 1.4 %add_convert_fusion = f32[2]{0:T(128)S(1)} fusion(pred[1]{0:T(512)(128)(4,1)} %bitcast.2, pred[1]{0:T(512)(128)(4,1)} %bitcast.1), kind=kLoop, calls=%fused_computation.42 | loop fusion | flops 4 | bytes 10 | tf_op jit(solution)/shard_map/convert_element_type | solution.py:418
  3.4 0.0 copy-start.1
  3.4 0.0 copy-start.6
  3.4 1.7 %fusion = f32[384]{0:T(512)S(1)} fusion(bf16[1,384,1536]{2,1,0:T(8,128)(2,1)} %param.7), kind=kLoop, calls=%fused_computation.10 | loop fusion | flops 1769088 | bytes 1181184 | tf_op jit(solution)/shard_map/reduce_sum | solution.py:406
  5.1 1.6 %fusion.9 = f32[384]{0:T(512)S(1)} fusion(bf16[1,384,1536]{2,1,0:T(8,128)(2,1)} %param.8), kind=kLoop, calls=%fused_computation.19 | loop fusion | flops 1769088 | bytes 1181184 | tf_op jit(solution)/shard_map/reduce_sum | solution.py:406
  6.7 2.6 %all-reduce = (f32[384]{0:T(512)S(1)}, f32[384]{0:T(512)S(1)}) all-reduce(f32[384]{0:T(512)S(1)} %fusion, f32[384]{0:T(512)S(1)} %fusion.9), channel_id=1, replica_groups=mesh['batch'=4,'tm'=4,'tensor'=2] {'tensor'}, use_global_device_ids=true, to_apply=%region_1.0 | all-reduce | flops 768 | bytes 6144 | tf_op jit(solution)/shard_map/psum | solution.py:405
  9.3 0.7 broadcast_in_dim.8.refs_0_
  10.0 0.0 copy-done
  10.0 0.0 copy-done.5
  10.0 1.3 %fusion.11.refs_2_ = bf16[384,1536]{1,0:T(8,128)(2,1)} fusion(bf16[1,384,1536]{2,1,0:T(8,128)(2,1)S(1)} %copy-done, f32[1536]{0:T(1024)S(1)} %copy-done.5, f32[384]{0:T(512)S(1)} %add_rsqrt_fusion), kind=kLoop, calls=%fused_computation.21 | loop fusion | flops 2359296 | bytes 2366976 | tf_op jit(solution)/shard_map/convert_element_type | solution.py:411
  11.3 0.0 copy-done.1
  11.3 0.0 copy-done.6
  11.3 1.4 %fusion.2.refs_1_ = bf16[384,1536]{1,0:T(8,128)(2,1)} fusion(bf16[1,384,1536]{2,1,0:T(8,128)(2,1)S(1)} %copy-done.1, f32[1536]{0:T(1024)S(1)} %copy-done.6, f32[384]{0:T(512)S(1)} %add_rsqrt_fusion.1), kind=kLoop, calls=%fused_computation.12 | loop fusion | flops 2359296 | bytes 2366976 | tf_op jit(solution)/shard_map/convert_element_type | solution.py:410
  12.7 90.7 %attention.1 = (f32[384,1536]{1,0:T(8,128)}, f32[384,1536]{1,0:T(8,128)}, bf16[384,1536]{1,0:T(8,128)(2,1)}) custom-call(f32[2,384]{1,0:T(2,128)} %broadcast_in_dim.8.refs_0_, bf16[384,1536]{1,0:T(8,128)(2,1)} %fusion.2.refs_1_, bf16[384,1536]{1,0:T(8,128)(2,1)} %fusion.11.refs_2_, bf16[384,1536]{1,0:T(8,128)(2,1)} %bitcast.24, bf16[384,1536]{1,0:T(8,128)(2,1)} %bitcast.25), custom_call_target="tpu_custom_call" | custom-call | tf_op jit(solution)/shard_map/attention/pallas_call | solution.py:262
  103.4 0.0 copy-start.3
  103.4 2.5 %fusion.6 = (f32[384]{0:T(512)S(1)}, f32[1536]{0:T(1024)S(1)}) fusion(f32[384,1536]{1,0:T(8,128)} %get-tuple-element.10, bf16[1,384,1536]{2,1,0:T(8,128)(2,1)S(1)} %copy-done.1, f32[1536]{0:T(1024)S(1)} %copy-done.6, f32[384]{0:T(512)S(1)} %add_rsqrt_fusion.1), kind=kLoop, calls=%fused_computation.16 | loop fusion | flops 4126848 | bytes 3554304 | tf_op jit(solution)/shard_map/reduce_sum | solution.py:430
  105.9 0.0 copy-done.3
  106.0 0.7 fusion.15
  106.6 0.6 pad_maximum_fusion.1.proj
  107.2 0.6 pad_maximum_fusion.gains
  107.9 10.4 %totals.1 = (f32[2,1536]{1,0:T(2,128)}, f32[2,384]{1,0:T(2,128)}) custom-call(f32[2,1536]{1,0:T(2,128)} %pad_maximum_fusion.gains, f32[2,384]{1,0:T(2,128)} %pad_maximum_fusion.1.proj), custom_call_target="tpu_custom_call" | custom-call | tf_op jit(solution)/shard_map/totals/pallas_call | solution.py:369
  118.2 0.8 slice_reduce_fusion
  119.0 0.0 copy-start.2
  119.0 3.3 %fusion.18 = bf16[1,384,1536]{2,1,0:T(8,128)(2,1)} fusion(f32[384,1536]{1,0:T(8,128)} %get-tuple-element.11, bf16[1,384,1536]{2,1,0:T(8,128)(2,1)S(1)} %copy-done, f32[384]{0:T(512)S(1)} %get-tuple-element.28, f32[1536]{0:T(1024)S(1)} %copy-done.5, f32[384]{0:T(512)S(1)} %add_rsqrt_fusion), kind=kLoop, calls=%fused_computation.28 | loop fusion | flops 3538944 | bytes 4727808 | tf_op jit(solution)/shard_map/broadcast_in_dim | solution.py:440
  122.4 0.0 copy-done.2
  122.4 0.0 copy-start.7
  122.4 0.0 copy-start.4
  122.4 1.5 %fusion.19 = bf16[1,384,1536]{2,1,0:T(8,128)(2,1)} fusion(f32[384,1536]{1,0:T(8,128)S(1)} %copy-done.2, bf16[1,384,1536]{2,1,0:T(8,128)(2,1)S(1)} %copy-done.1, f32[384]{0:T(512)S(1)} %get-tuple-element.27, f32[1536]{0:T(1024)S(1)} %copy-done.6, f32[384]{0:T(512)S(1)} %add_rsqrt_fusion.1), kind=kLoop, calls=%fused_computation.29 | loop fusion | flops 3538944 | bytes 4727808 | tf_op jit(solution)/shard_map/broadcast_in_dim | solution.py:439
  123.9 0.0 copy-done.7
  123.9 0.6 multiply_reduce_fusion
  124.5 0.0 copy-done.4
  124.5 1.0 copy.13
  (7 shorter events, 0.0 us)
Async XLA Ops:
  0.6 9.3 %copy-start = (bf16[1,384,1536]{2,1,0:T(8,128)(2,1)S(1)}, bf16[1,384,1536]{2,1,0:T(8,128)(2,1)}, u32[]{:S(2)}) copy-start(bf16[1,384,1536]{2,1,0:T(8,128)(2,1)} %param.8) | copy-start | bytes 3538948
  0.6 9.3 %copy-start.5 = (f32[1536]{0:T(1024)S(1)}, f32[1536]{0:T(1024)}, u32[]{:S(2)}) copy-start(f32[1536]{0:T(1024)} %param.12) | copy-start | bytes 18436
  3.4 7.9 %copy-start.1 = (bf16[1,384,1536]{2,1,0:T(8,128)(2,1)S(1)}, bf16[1,384,1536]{2,1,0:T(8,128)(2,1)}, u32[]{:S(2)}) copy-start(bf16[1,384,1536]{2,1,0:T(8,128)(2,1)} %param.7) | copy-start | bytes 3538948
  3.4 7.9 %copy-start.6 = (f32[1536]{0:T(1024)S(1)}, f32[1536]{0:T(1024)}, u32[]{:S(2)}) copy-start(f32[1536]{0:T(1024)} %param.11) | copy-start | bytes 18436
  103.4 2.5 %copy-start.3 = (f32[384,1536]{1,0:T(8,128)S(1)}, f32[384,1536]{1,0:T(8,128)}, u32[]{:S(2)}) copy-start(f32[384,1536]{1,0:T(8,128)} %get-tuple-element.11) | copy-start | bytes 7077892
  119.0 3.3 %copy-start.2 = (f32[384,1536]{1,0:T(8,128)S(1)}, f32[384,1536]{1,0:T(8,128)}, u32[]{:S(2)}) copy-start(f32[384,1536]{1,0:T(8,128)} %get-tuple-element.10) | copy-start | bytes 7077892
  122.4 1.5 %copy-start.7 = (f32[2,1536]{1,0:T(2,128)S(1)}, f32[2,1536]{1,0:T(2,128)}, u32[]{:S(2)}) copy-start(f32[2,1536]{1,0:T(2,128)} %get-tuple-element.14) | copy-start | bytes 36868
  122.4 2.2 %copy-start.4 = (bf16[384,1536]{1,0:T(8,128)(2,1)S(1)}, bf16[384,1536]{1,0:T(8,128)(2,1)}, u32[]{:S(2)}) copy-start(bf16[384,1536]{1,0:T(8,128)(2,1)} %get-tuple-element.13) | copy-start | bytes 3538948

commit v3 on v2

--- a/solution.py
+++ b/solution.py
@@ -38,11 +38,13 @@
     return highest, total, weighted
 
 
-def attention_body(group, chunks, live, q, k, v, g, dq, dk, dv,
-                   rq, rg, st_own, st_out, st_in, co_own, co_out, co_in, dq_out, dq_in,
+def attention_body(group, chunks, entries, q_raw, k_raw, v, g, gain_q, gain_k, dq, dk, dv, inv,
+                   q, k, squares, sq_send, sq_recv, rq, rg, st_own, st_out, st_in, co_own, co_out, co_in, dq_out, dq_in,
                    bulk_send, bulk_recv, st_send, st_recv, co_send, co_recv, dq_send, dq_recv):
-    rows = q.shape[0]
+    rows, width = q.shape
     span = group * HD
+    core = lax.axis_index("tensor")
+    cores = lax.axis_size("tensor")
     me = lax.axis_index("tm")
     peers = lax.axis_size("tm")
     has = (me > 0, me < peers - 1)
@@ -57,13 +59,23 @@
             device_id={"tm": target[side]}, device_id_type=MESH,
         )
 
+    def grad_copy(chunk, side, slot):
+        where = part(chunk)
+        return remote(g.at[:, where], rg.at[slot, :, where],
+                      bulk_send.at[side, 0, chunk], bulk_recv.at[slot, 0, chunk], side)
+
+    def query_copy(chunk, side, slot):
+        where = part(chunk)
+        return remote(q.at[:, where], rq.at[slot, :, where],
+                      bulk_send.at[side, 1, chunk], bulk_recv.at[slot, 1, chunk], side)
+
     def bulk(chunk, side, slot):
-        where = part(chunk)
-        return (
-            remote(g.at[:, where], rg.at[slot, :, where],
-                   bulk_send.at[side, 0, chunk], bulk_recv.at[slot, 0, chunk], side),
-            remote(q.at[:, where], rq.at[slot, :, where],
-                   bulk_send.at[side, 1, chunk], bulk_recv.at[slot, 1, chunk], side),
+        return grad_copy(chunk, side, slot), query_copy(chunk, side, slot)
+
+    def square_copy(slot, peer):
+        return pltpu.make_async_remote_copy(
+            src_ref=squares.at[slot], dst_ref=squares.at[slot], send_sem=sq_send.at[peer],
+            recv_sem=sq_recv.at[slot], device_id={"tensor": peer}, device_id_type=MESH,
         )
 
     def small(out, into, send, recv, chunk, side, slot):
@@ -87,17 +99,60 @@
         @pl.when(has[side])
         def _():
             pl.semaphore_signal(barrier, inc=1, device_id={"tm": target[side]}, device_id_type=MESH)
-    pl.semaphore_wait(barrier, (me > 0).astype(jnp.int32) + (me < peers - 1).astype(jnp.int32))
-
-    def start_bulk(chunk):
+    for i in range(1, cores):
+        pl.semaphore_signal(
+            barrier, inc=1, device_id={"tensor": lax.rem(core + i, cores)}, device_id_type=MESH)
+    neighbours = (me > 0).astype(jnp.int32) + (me < peers - 1).astype(jnp.int32)
+    pl.semaphore_wait(barrier, neighbours + (cores - 1))
+
+    def start_each(make, chunk):
         for side in range(2):
             @pl.when(has[side])
             def _():
-                for copy in bulk(chunk, side, 1 - side):
-                    copy.start()
+                make(chunk, side, 1 - side).start()
+
+    def start_bulk(chunk):
+        start_each(grad_copy, chunk)
+        start_each(query_copy, chunk)
 
     for chunk in range(min(2, chunks)):
-        start_bulk(chunk)
+        start_each(grad_copy, chunk)
+
+    block = math.gcd(rows, 128)
+    for index, raw in enumerate((q_raw, k_raw)):
+        for top in range(0, rows, block):
+            total = jnp.zeros((block, HD), jnp.float32)
+            for left in range(0, width, HD):
+                wide = raw[top:top + block, left:left + HD].astype(jnp.float32)
+                total = total + wide * wide
+            squares[core, index, top:top + block, :] = total
+    for i in range(1, cores):
+        square_copy(core, lax.rem(core + i, cores)).start()
+    for i in range(1, cores):
+        peer = lax.rem(core + i, cores)
+        square_copy(core, peer).wait_send()
+        square_copy(peer, peer).wait_recv()
+    for index, (raw, gain, out) in enumerate(((q_raw, gain_q, q), (k_raw, gain_k, k))):
+        for top in range(0, rows, block):
+            total = squares[0, index, top:top + block, :]
+            for other in range(1, cores):
+                total = total + squares[other, index, top:top + block, :]
+            mean = jnp.sum(total, axis=1, keepdims=True) / (width * cores)
+            inverse = jnp.broadcast_to(lax.rsqrt(mean + EPSILON), (block, HD))
+            inv[index, top:top + block, :] = inverse
+            for left in range(0, width, HD):
+                wide = raw[top:top + block, left:left + HD].astype(jnp.float32)
+                out[top:top + block, left:left + HD] = (
+                    wide * inverse * gain[:, left:left + HD]
+                ).astype(out.dtype)
+    for chunk in range(min(2, chunks)):
+        start_each(query_copy, chunk)
+    alive = tuple(
+        has[side] & (
+            (entries[0] == target[side]) | (entries[1] == target[side])
+            | (entries[2] == target[side]))
+        for side in range(2)
+    )
     for side in range(2):
         @pl.when(jnp.logical_not(has[side]))
         def _():
@@ -136,7 +191,6 @@
                 def _():
                     stat_copy(s - 1, side, side).wait_recv()
             where = pl.ds((s - 1) * group, group)
-            alive = (live[0:1, :] > 0.5, live[1:2, :] > 0.5)
             highest = st_own[where, 0:1, :]
             for side in range(2):
                 highest = jnp.where(
@@ -247,11 +301,12 @@
     lax.fori_loop(0, chunks, drain, 0)
 
 
-def attention(live, query, key, value, grad):
+def attention(entries, query, key, value, grad, gain_q, gain_k):
     rows, width = query.shape
     heads = width // HD
     group = math.gcd(GROUP, heads)
     chunks = heads // group
+    cores = lax.axis_size("tensor")
     whole = pl.BlockSpec(memory_space=pltpu.VMEM)
     stat = (heads, STATS, rows)
     dma = pltpu.SemaphoreType.DMA
@@ -265,10 +320,15 @@
             jax.ShapeDtypeStruct((rows, width), jnp.float32),
             jax.ShapeDtypeStruct((rows, width), jnp.float32),
             jax.ShapeDtypeStruct((rows, width), jnp.bfloat16),
+            jax.ShapeDtypeStruct((2, rows, HD), jnp.float32),
         ],
-        in_specs=[whole] * 5,
-        out_specs=[whole] * 3,
+        in_specs=[pl.BlockSpec(memory_space=pltpu.SMEM)] + [whole] * 6,
+        out_specs=[whole] * 4,
         scratch_shapes=[
+            pltpu.VMEM((rows, width), jnp.bfloat16),
+            pltpu.VMEM((rows, width), jnp.bfloat16),
+            pltpu.VMEM((cores, 2, rows, HD), jnp.float32),
+            dma((cores,)), dma((cores,)),
             pltpu.VMEM((2, rows, width), jnp.bfloat16),
             pltpu.VMEM((2, rows, width), jnp.bfloat16),
             pltpu.VMEM(stat, jnp.float32),
@@ -286,7 +346,7 @@
         ],
         compiler_params=pltpu.CompilerParams(collective_id=0, has_side_effects=True),
         name="attention",
-    )(live, query, key, value, grad)
+    )(entries, query, key, value, grad, gain_q, gain_k)
 
 
 def totals_body(gains, proj, gain_sum, proj_sum, gain_slots, proj_slots,
@@ -402,22 +462,11 @@
     token_count, feature_count = query_wide.shape
     width_all = feature_count * lax.axis_size("tensor")
     count_all = lax.axis_size("batch") * lax.axis_size("tm") * token_count
-    squares = lax.psum(
-        (jnp.sum(query_wide * query_wide, axis=1), jnp.sum(key_wide * key_wide, axis=1)), "tensor"
-    )
-    inverse_q = lax.rsqrt(squares[0] / width_all + EPSILON)
-    inverse_k = lax.rsqrt(squares[1] / width_all + EPSILON)
-    query_norm = (query_wide * inverse_q[:, None] * gain_q[None, :]).astype(jnp.bfloat16)
-    key_norm = (key_wide * inverse_k[:, None] * gain_k[None, :]).astype(jnp.bfloat16)
-    position = lax.axis_index("tm")
-    live = jnp.stack(
-        [
-            jnp.any((entries >= 0) & (entries == position - 1)),
-            jnp.any((entries >= 0) & (entries == position + 1)),
-        ]
-    ).astype(jnp.float32)
-    live = jnp.broadcast_to(live[:, None], (2, token_count))
-    grad_query, grad_kn, grad_values = attention(live, query_norm, key_norm, value_rows, grad_rows)
+    grad_query, grad_kn, grad_values, inverse = attention(
+        entries, q_raw[0], k_raw[0], value_rows, grad_rows, gain_q[None], gain_k[None]
+    )
+    inverse_q = inverse[0, :, 0]
+    inverse_k = inverse[1, :, 0]
     gain_terms, proj = totals(
         jnp.stack(
             [

time: 126 us -> 119 us (0.944)
  other arithmetic: 18.6 us -> 10.4 us
  local copies, waits for them, and re-layouts: 2.49 us -> 5.61 us
  blocking collectives: 2.62 us -> 0 us
    convert_element_type x3 -> x0, other arithmetic: 4.07 us -> none  [the longest x1 1.37 us: shards(): live = jnp.stack([jnp.any((entries >= 0) & (entries == position - 1)), jn...]
    reduce_sum x3 -> x0, other arithmetic: 3.93 us -> none  [the longest x1 1.67 us: shards(): jnp.sum(query_wide * query_wide, axis=1)]
    psum x1 -> x0, blocking collectives: 2.62 us -> none  [shards(): lax.psum((jnp.sum(query_wide * query_wide, axis=1), jnp.sum(key_wide * ke...]
    broadcast_in_dim x1 -> x2, local copies, waits for them, and re-layouts: 0.66 us -> 2.59 us  [the longest x1 1.3 us: shards(): gain_q[None]]
    reduce_or x1 -> x0, other arithmetic: 1.39 us -> none  [shards(): jnp.any((entries >= 0) & (entries == position - 1))]
where the time goes in v3:
time: 119 us
  Pallas kernels  102 us (86%)
  other arithmetic  10.4 us (9%)
  local copies, waits for them, and re-layouts  5.61 us (5%)
    pallas_call x1, Pallas kernels, attention(): pl.pallas_call(body, out_shape=[jax.ShapeDtypeStruct((rows, width), jnp.f...  91.5 us
    pallas_call x1, Pallas kernels, totals(): pl.pallas_call(totals_body, out_shape=[jax.ShapeDtypeStruct(gains.shape,...  10.4 us
    reduce_sum x1, other arithmetic, shards(): jnp.sum(query_wide * gain_q[None, :] * grad_query, axis=1)  3.73 us
    broadcast_in_dim x1, other arithmetic, shards(): grad_k[None]  3.34 us

profile of v3, /device:TPU:0, one launch (start us, length us, event | category | flops | bytes accessed | tf_op | source)
XLA Modules:
  0.0 118.7 jit_solution(10657813401213354684)
XLA Ops:
  0.6 1.3 %broadcast_in_dim.10.refs_5_ = f32[1,1536]{1,0:T(1,128)} reshape(f32[1536]{0:T(1024)} %param.11) | data formatting | bytes 12288 | tf_op jit(solution)/shard_map/broadcast_in_dim | solution.py:466
  1.9 1.3 %broadcast_in_dim.22.refs_6_ = f32[1,1536]{1,0:T(1,128)} reshape(f32[1536]{0:T(1024)} %param.12) | data formatting | bytes 12288 | tf_op jit(solution)/shard_map/broadcast_in_dim | solution.py:466
  3.2 0.0 copy-start
  3.2 0.0 copy-start.1
  3.2 0.0 copy-start.4
  3.2 0.0 copy-start.5
  3.2 91.5 %attention.1 = (f32[384,1536]{1,0:T(8,128)}, f32[384,1536]{1,0:T(8,128)}, bf16[384,1536]{1,0:T(8,128)(2,1)}, f32[2,384,128]{2,1,0:T(8,128)}) custom-call(s32[3]{0:T(128)} %bitcast.21, bf16[384,1536]{1,0:T(8,128)(2,1)} %bitcast.17, bf16[384,1536]{1,0:T(8,128)(2,1)} %bitcast.16, bf16[384,1536]{1,0:T(8,128)(2,1)} %bitcast.19, bf16[384,1536]{1,0:T(8,128)(2,1)} %bitcast.20, ...), custom_call_target="tpu_custom_call" | custom-call | tf_op jit(solution)/shard_map/attention/pallas_call | solution.py:317
  94.8 1.2 %slice_reduce_fusion.1 = (f32[384]{0:T(512)S(1)}, f32[384]{0:T(512)S(1)}) fusion(f32[2,384,128]{2,1,0:T(8,128)} %get-tuple-element.11), kind=kLoop, calls=%fused_computation.21 | loop fusion | bytes 6144 | tf_op jit(solution)/shard_map/slice | solution.py:468
  96.0 0.0 copy-done
  96.0 0.0 copy-done.1
  96.0 0.0 copy-done.4
  96.0 0.0 copy-done.5
  96.0 3.7 %fusion.3 = (f32[384]{0:T(512)S(1)}, f32[1536]{0:T(1024)S(1)}, f32[1536]{0:T(1024)S(1)}, f32[384]{0:T(512)S(1)}) fusion(f32[384,1536]{1,0:T(8,128)} %get-tuple-element.12, f32[1536]{0:T(1024)S(1)} %copy-done.5, bf16[1,384,1536]{2,1,0:T(8,128)(2,1)S(1)} %copy-done.1, f32[384]{0:T(512)S(1)} %get-tuple-element.21, f32[384]{0:T(512)S(1)} %get-tuple-element.22, ...), kind=kLoop, calls=%fused_computation.9 | loop fusion | flops 8253696 | bytes 7108608 | tf_op jit(solution)/shard_map/reduce_sum | solution.py:479
  99.8 0.6 pad_maximum_fusion.1.proj
  100.4 0.6 pad_maximum_fusion.gains
  101.0 10.4 %totals.1 = (f32[2,1536]{1,0:T(2,128)}, f32[2,384]{1,0:T(2,128)}) custom-call(f32[2,1536]{1,0:T(2,128)} %pad_maximum_fusion.gains, f32[2,384]{1,0:T(2,128)} %pad_maximum_fusion.1.proj), custom_call_target="tpu_custom_call" | custom-call | tf_op jit(solution)/shard_map/totals/pallas_call | solution.py:429
  111.4 0.8 slice_reduce_fusion.2
  112.1 0.0 copy-start.2
  112.1 3.3 %fusion.12 = bf16[1,384,1536]{2,1,0:T(8,128)(2,1)} fusion(f32[384,1536]{1,0:T(8,128)} %get-tuple-element.13, f32[384]{0:T(512)S(1)} %fusion.17, f32[1536]{0:T(1024)S(1)} %copy-done.4, f32[384]{0:T(512)S(1)} %get-tuple-element.22, bf16[1,384,1536]{2,1,0:T(8,128)(2,1)S(1)} %copy-done), kind=kLoop, calls=%fused_computation.18 | loop fusion | flops 3538944 | bytes 4727808 | tf_op jit(solution)/shard_map/broadcast_in_dim | solution.py:489
  115.5 0.0 copy-done.2
  115.5 0.0 copy-start.6
  115.5 0.0 copy-start.3
  115.5 1.5 %fusion.13 = bf16[1,384,1536]{2,1,0:T(8,128)(2,1)} fusion(f32[384,1536]{1,0:T(8,128)S(1)} %copy-done.2, f32[384]{0:T(512)S(1)} %fusion.15, f32[1536]{0:T(1024)S(1)} %copy-done.5, f32[384]{0:T(512)S(1)} %get-tuple-element.21, bf16[1,384,1536]{2,1,0:T(8,128)(2,1)S(1)} %copy-done.1), kind=kLoop, calls=%fused_computation.19 | loop fusion | flops 3538944 | bytes 4727808 | tf_op jit(solution)/shard_map/broadcast_in_dim | solution.py:488
  117.0 0.0 copy-done.6
  117.0 0.6 multiply_reduce_fusion
  117.7 0.0 copy-done.3
  117.7 1.0 copy.13
  (6 shorter events, 0.0 us)
Async XLA Ops:
  3.2 92.8 %copy-start = (bf16[1,384,1536]{2,1,0:T(8,128)(2,1)S(1)}, bf16[1,384,1536]{2,1,0:T(8,128)(2,1)}, u32[]{:S(2)}) copy-start(bf16[1,384,1536]{2,1,0:T(8,128)(2,1)} %param.8) | copy-start | bytes 3538948
  3.2 92.8 %copy-start.1 = (bf16[1,384,1536]{2,1,0:T(8,128)(2,1)S(1)}, bf16[1,384,1536]{2,1,0:T(8,128)(2,1)}, u32[]{:S(2)}) copy-start(bf16[1,384,1536]{2,1,0:T(8,128)(2,1)} %param.7) | copy-start | bytes 3538948
  3.2 92.8 %copy-start.4 = (f32[1536]{0:T(1024)S(1)}, f32[1536]{0:T(1024)}, u32[]{:S(2)}) copy-start(f32[1536]{0:T(1024)} %param.12) | copy-start | bytes 18436
  3.2 92.8 %copy-start.5 = (f32[1536]{0:T(1024)S(1)}, f32[1536]{0:T(1024)}, u32[]{:S(2)}) copy-start(f32[1536]{0:T(1024)} %param.11) | copy-start | bytes 18436
  112.1 3.4 %copy-start.2 = (f32[384,1536]{1,0:T(8,128)S(1)}, f32[384,1536]{1,0:T(8,128)}, u32[]{:S(2)}) copy-start(f32[384,1536]{1,0:T(8,128)} %get-tuple-element.12) | copy-start | bytes 7077892
  115.5 1.5 %copy-start.6 = (f32[2,1536]{1,0:T(2,128)S(1)}, f32[2,1536]{1,0:T(2,128)}, u32[]{:S(2)}) copy-start(f32[2,1536]{1,0:T(2,128)} %get-tuple-element.16) | copy-start | bytes 36868
  115.5 2.2 %copy-start.3 = (bf16[384,1536]{1,0:T(8,128)(2,1)S(1)}, bf16[384,1536]{1,0:T(8,128)(2,1)}, u32[]{:S(2)}) copy-start(bf16[384,1536]{1,0:T(8,128)(2,1)} %get-tuple-element.15) | copy-start | bytes 3538948

commit v4 on v3

--- a/solution.py
+++ b/solution.py
@@ -38,7 +38,9 @@
     return highest, total, weighted
 
 
-def attention_body(group, chunks, entries, q_raw, k_raw, v, g, gain_q, gain_k, dq, dk, dv, inv,
+def attention_body(group, chunks, entries, q_raw, k_raw, v, g, gain_q, gain_k,
+                   grad_q, grad_k, dv, gain_sum,
+                   dq, dk, inv, proj, terms, pj_send, pj_recv, tm_send, tm_recv,
                    q, k, squares, sq_send, sq_recv, rq, rg, st_own, st_out, st_in, co_own, co_out, co_in, dq_out, dq_in,
                    bulk_send, bulk_recv, st_send, st_recv, co_send, co_recv, dq_send, dq_recv):
     rows, width = q.shape
@@ -94,16 +96,39 @@
         return remote(dq_out.at[side, :, where], dq_in.at[slot, :, where],
                       dq_send.at[side, chunk], dq_recv.at[slot, chunk], side)
 
+    count = lax.axis_size("batch") * peers
+    rank = lax.axis_index("batch") * peers + me
+
+    def other_rank(i):
+        return lax.rem(rank + i, count)
+
+    def rank_id(peer):
+        return {"batch": lax.div(peer, peers), "tm": lax.rem(peer, peers)}
+
+    def proj_copy(slot, peer):
+        return pltpu.make_async_remote_copy(
+            src_ref=proj.at[slot], dst_ref=proj.at[slot], send_sem=pj_send.at[peer],
+            recv_sem=pj_recv.at[slot], device_id={"tensor": peer}, device_id_type=MESH,
+        )
+
+    def term_copy(slot, peer):
+        return pltpu.make_async_remote_copy(
+            src_ref=terms.at[slot], dst_ref=terms.at[slot], send_sem=tm_send.at[peer],
+            recv_sem=tm_recv.at[slot], device_id=rank_id(peer), device_id_type=MESH,
+        )
+
     barrier = pltpu.get_barrier_semaphore()
-    for side in range(2):
-        @pl.when(has[side])
-        def _():
-            pl.semaphore_signal(barrier, inc=1, device_id={"tm": target[side]}, device_id_type=MESH)
+
+    def greet(i, carry):
+        pl.semaphore_signal(
+            barrier, inc=1, device_id=rank_id(other_rank(i)), device_id_type=MESH)
+        return carry
+
+    lax.fori_loop(1, count, greet, 0)
     for i in range(1, cores):
         pl.semaphore_signal(
             barrier, inc=1, device_id={"tensor": lax.rem(core + i, cores)}, device_id_type=MESH)
-    neighbours = (me > 0).astype(jnp.int32) + (me < peers - 1).astype(jnp.int32)
-    pl.semaphore_wait(barrier, neighbours + (cores - 1))
+    pl.semaphore_wait(barrier, count - 1 + cores - 1)
 
     def start_each(make, chunk):
         for side in range(2):
@@ -143,7 +168,7 @@
             for left in range(0, width, HD):
                 wide = raw[top:top + block, left:left + HD].astype(jnp.float32)
                 out[top:top + block, left:left + HD] = (
-                    wide * inverse * gain[:, left:left + HD]
+                    wide * inverse * gain[left // HD:left // HD + 1, :]
                 ).astype(out.dtype)
     for chunk in range(min(2, chunks)):
         start_each(query_copy, chunk)
@@ -299,6 +324,55 @@
         return carry
 
     lax.fori_loop(0, chunks, drain, 0)
+    heads = width // HD
+    sides = ((q_raw, gain_q, dq, grad_q), (k_raw, gain_k, dk, grad_k))
+    for index, (raw, gain, normed, out) in enumerate(sides):
+        proj[core, index] = jnp.zeros((rows, HD), jnp.float32)
+
+        def reduce(head, carry):
+            col = column(head)
+            both = raw[:, col].astype(jnp.float32) * normed[:, col]
+            terms[rank, index, pl.ds(head, 1), :] = jnp.sum(
+                both * inv[index], axis=0, keepdims=True)
+            proj[core, index] = proj[core, index] + both * gain[pl.ds(head, 1), :]
+            return carry
+
+        lax.fori_loop(0, heads, reduce, 0)
+    for i in range(1, cores):
+        proj_copy(core, lax.rem(core + i, cores)).start()
+
+    def send_terms(i, carry):
+        term_copy(rank, other_rank(i)).start()
+        return carry
+
+    lax.fori_loop(1, count, send_terms, 0)
+    for i in range(1, cores):
+        peer = lax.rem(core + i, cores)
+        proj_copy(core, peer).wait_send()
+        proj_copy(peer, peer).wait_recv()
+    for index, (raw, gain, normed, out) in enumerate(sides):
+        for top in range(0, rows, block):
+            total = proj[0, index, top:top + block, :]
+            for other in range(1, cores):
+                total = total + proj[other, index, top:top + block, :]
+            inverse = inv[index, top:top + block, :]
+            projection = jnp.sum(total, axis=1, keepdims=True)
+            pull = inverse * inverse * inverse * projection / (width * cores)
+            for left in range(0, width, HD):
+                wide = raw[top:top + block, left:left + HD].astype(jnp.float32)
+                out[top:top + block, left:left + HD] = (
+                    inverse * gain[left // HD:left // HD + 1, :]
+                    * normed[top:top + block, left:left + HD] - wide * pull
+                ).astype(out.dtype)
+
+    def end_terms(i, carry):
+        peer = other_rank(i)
+        term_copy(rank, peer).wait_send()
+        term_copy(peer, peer).wait_recv()
+        return carry
+
+    lax.fori_loop(1, count, end_terms, 0)
+    gain_sum[...] = jnp.sum(terms[...], axis=0) * (1.0 / math.sqrt(count * rows))
 
 
 def attention(entries, query, key, value, grad, gain_q, gain_k):
@@ -307,6 +381,7 @@
     group = math.gcd(GROUP, heads)
     chunks = heads // group
     cores = lax.axis_size("tensor")
+    count = lax.axis_size("batch") * lax.axis_size("tm")
     whole = pl.BlockSpec(memory_space=pltpu.VMEM)
     stat = (heads, STATS, rows)
     dma = pltpu.SemaphoreType.DMA
@@ -317,14 +392,20 @@
     return pl.pallas_call(
         body,
         out_shape=[
-            jax.ShapeDtypeStruct((rows, width), jnp.float32),
-            jax.ShapeDtypeStruct((rows, width), jnp.float32),
             jax.ShapeDtypeStruct((rows, width), jnp.bfloat16),
-            jax.ShapeDtypeStruct((2, rows, HD), jnp.float32),
+            jax.ShapeDtypeStruct((rows, width), jnp.bfloat16),
+            jax.ShapeDtypeStruct((rows, width), jnp.bfloat16),
+            jax.ShapeDtypeStruct((2, heads, HD), jnp.float32),
         ],
         in_specs=[pl.BlockSpec(memory_space=pltpu.SMEM)] + [whole] * 6,
         out_specs=[whole] * 4,
         scratch_shapes=[
+            pltpu.VMEM((rows, width), jnp.float32),
+            pltpu.VMEM((rows, width), jnp.float32),
+            pltpu.VMEM((2, rows, HD), jnp.float32),
+            pltpu.VMEM((cores, 2, rows, HD), jnp.float32),
+            pltpu.VMEM((count, 2, heads, HD), jnp.float32),
+            dma((cores,)), dma((cores,)), dma((count,)), dma((count,)),
             pltpu.VMEM((rows, width), jnp.bfloat16),
             pltpu.VMEM((rows, width), jnp.bfloat16),
             pltpu.VMEM((cores, 2, rows, HD), jnp.float32),
@@ -349,147 +430,19 @@
     )(entries, query, key, value, grad, gain_q, gain_k)
 
 
-def totals_body(gains, proj, gain_sum, proj_sum, gain_slots, proj_slots,
-                gain_send, gain_recv, proj_send, proj_recv):
-    tm = lax.axis_size("tm")
-    count = lax.axis_size("batch") * tm
-    me = lax.axis_index("batch") * tm + lax.axis_index("tm")
-    cores = lax.axis_size("tensor")
-    core = lax.axis_index("tensor")
-    barrier = pltpu.get_barrier_semaphore()
-
-    def gain_peer(i):
-        return lax.rem(me + i, count)
-
-    def gain_id(peer):
-        return {"batch": lax.div(peer, tm), "tm": lax.rem(peer, tm)}
-
-    def core_peer(i):
-        return lax.rem(core + i, cores)
-
-    def greet_gain(i, carry):
-        pl.semaphore_signal(barrier, inc=1, device_id=gain_id(gain_peer(i)), device_id_type=MESH)
-        return carry
-
-    def greet_core(i, carry):
-        pl.semaphore_signal(barrier, inc=1, device_id={"tensor": core_peer(i)}, device_id_type=MESH)
-        return carry
-
-    lax.fori_loop(1, count, greet_gain, 0)
-    lax.fori_loop(1, cores, greet_core, 0)
-    gain_slots[me] = gains[...]
-    proj_slots[core] = proj[...]
-    pl.semaphore_wait(barrier, count - 1 + cores - 1)
-
-    def gain_copy(slot, peer):
-        return pltpu.make_async_remote_copy(
-            src_ref=gains, dst_ref=gain_slots.at[slot], send_sem=gain_send.at[peer],
-            recv_sem=gain_recv.at[slot], device_id=gain_id(peer), device_id_type=MESH,
-        )
-
-    def proj_copy(slot, peer):
-        return pltpu.make_async_remote_copy(
-            src_ref=proj, dst_ref=proj_slots.at[slot], send_sem=proj_send.at[peer],
-            recv_sem=proj_recv.at[slot], device_id={"tensor": peer}, device_id_type=MESH,
-        )
-
-    def send_core(i, carry):
-        proj_copy(core, core_peer(i)).start()
-        return carry
-
-    def send_gain(i, carry):
-        gain_copy(me, gain_peer(i)).start()
-        return carry
-
-    def end_core(i, carry):
-        peer = core_peer(i)
-        proj_copy(core, peer).wait_send()
-        proj_copy(peer, peer).wait_recv()
-        return carry
-
-    def end_gain(i, carry):
-        peer = gain_peer(i)
-        gain_copy(me, peer).wait_send()
-        gain_copy(peer, peer).wait_recv()
-        return carry
-
-    lax.fori_loop(1, cores, send_core, 0)
-    lax.fori_loop(1, count, send_gain, 0)
-    lax.fori_loop(1, cores, end_core, 0)
-    lax.fori_loop(1, count, end_gain, 0)
-    proj_sum[...] = jnp.sum(proj_slots[...], axis=0)
-    gain_sum[...] = jnp.sum(gain_slots[...], axis=0)
-
-
-def totals(gains, proj):
-    count = lax.axis_size("batch") * lax.axis_size("tm")
-    cores = lax.axis_size("tensor")
-    whole = pl.BlockSpec(memory_space=pltpu.VMEM)
-    dma = pltpu.SemaphoreType.DMA
-    return pl.pallas_call(
-        totals_body,
-        out_shape=[
-            jax.ShapeDtypeStruct(gains.shape, jnp.float32),
-            jax.ShapeDtypeStruct(proj.shape, jnp.float32),
-        ],
-        in_specs=[whole] * 2,
-        out_specs=[whole] * 2,
-        scratch_shapes=[
-            pltpu.VMEM((count,) + gains.shape, jnp.float32),
-            pltpu.VMEM((cores,) + proj.shape, jnp.float32),
-            dma((count,)), dma((count,)), dma((cores,)), dma((cores,)),
-        ],
-        compiler_params=pltpu.CompilerParams(collective_id=1, has_side_effects=True),
-        name="totals",
-    )(gains, proj)
-
-
-def finish_norm(wide_rows, inverse, gain_row, grad_normed, projection, feature_count):
-    cubed = inverse * inverse * inverse
-    grad_rows = (
-        inverse[:, None] * gain_row[None, :] * grad_normed
-        - wide_rows * (cubed * projection / feature_count)[:, None]
-    )
-    return grad_rows.astype(jnp.bfloat16)
-
-
 def shards(q_raw, k_raw, values, grad_out, gain_q, gain_k, tile_lists):
-    query_wide = q_raw[0].astype(jnp.float32)
-    key_wide = k_raw[0].astype(jnp.float32)
-    value_rows = values[0]
-    grad_rows = grad_out[0]
-    entries = tile_lists[0, 0]
-    token_count, feature_count = query_wide.shape
-    width_all = feature_count * lax.axis_size("tensor")
-    count_all = lax.axis_size("batch") * lax.axis_size("tm") * token_count
-    grad_query, grad_kn, grad_values, inverse = attention(
-        entries, q_raw[0], k_raw[0], value_rows, grad_rows, gain_q[None], gain_k[None]
-    )
-    inverse_q = inverse[0, :, 0]
-    inverse_k = inverse[1, :, 0]
-    gain_terms, proj = totals(
-        jnp.stack(
-            [
-                jnp.sum(grad_query * query_wide * inverse_q[:, None], axis=0),
-                jnp.sum(grad_kn * key_wide * inverse_k[:, None], axis=0),
-            ]
-        ),
-        jnp.stack(
-            [
-                jnp.sum(query_wide * gain_q[None, :] * grad_query, axis=1),
-                jnp.sum(key_wide * gain_k[None, :] * grad_kn, axis=1),
-            ]
-        ),
-    )
-    grad_q = finish_norm(query_wide, inverse_q, gain_q, grad_query, proj[0], width_all)
-    grad_k = finish_norm(key_wide, inverse_k, gain_k, grad_kn, proj[1], width_all)
-    factor_all = 1.0 / math.sqrt(count_all)
+    width = q_raw.shape[2]
+    heads = width // HD
+    grad_q, grad_k, grad_values, gain_sum = attention(
+        tile_lists[0, 0], q_raw[0], k_raw[0], values[0], grad_out[0],
+        gain_q.reshape(heads, HD), gain_k.reshape(heads, HD),
+    )
     return (
         grad_q[None],
         grad_k[None],
         grad_values[None],
-        gain_terms[0] * factor_all,
-        gain_terms[1] * factor_all,
+        gain_sum[0].reshape(width),
+        gain_sum[1].reshape(width),
     )
 
 

time: 119 us -> 108 us (0.908)
  other arithmetic: 10.4 us -> 0 us
    broadcast_in_dim x2 -> x0, other arithmetic: 4.87 us -> none  [the longest x1 3.34 us: shards(): grad_k[None]]
    unnamed x15 -> x7, local copies, waits for them, and re-layouts: 1.04 us -> 5.17 us
    reduce_sum x1 -> x0, other arithmetic: 3.73 us -> none  [shards(): jnp.sum(query_wide * gain_q[None, :] * grad_query, axis=1)]
    broadcast_in_dim x2 -> x0, local copies, waits for them, and re-layouts: 2.59 us -> none  [the longest x1 1.3 us: shards(): gain_q[None]]
    slice x2 -> x0, local copies, waits for them, and re-layouts: 1.97 us -> none  [the longest x1 1.2 us: shards(): inverse_q = inverse[0, :, 0]]
    another operation x4 -> x1, local copies, waits for them, and re-layouts: 0.02 us -> 1.32 us  [shards(): gain_sum[1].reshape(width)]
    another operation x2 -> x0, other arithmetic: 1.2 us -> none  [the longest x1 0.61 us: shards(): jnp.stack([jnp.sum(grad_query * query_wide * inverse_q[:, None], axis=0),...]
    pallas_call x2 -> x1, Pallas kernels: 102 us -> 101 us  [attention(): pl.pallas_call(body, out_shape=[jax.ShapeDtypeStruct((rows, width), jnp.b...]
where the time goes in v4:
time: 108 us
  Pallas kernels  101 us (94%)
  local copies, waits for them, and re-layouts  6.49 us (6%)
    pallas_call x1, Pallas kernels, attention(): pl.pallas_call(body, out_shape=[jax.ShapeDtypeStruct((rows, width), jnp.b...  101 us
    unnamed x7, local copies, waits for them, and re-layouts  5.17 us

profile of v4, /device:TPU:0, one launch (start us, length us, event | category | flops | bytes accessed | tf_op | source)
XLA Modules:
  0.0 108.2 jit_solution(10051958164520921629)
XLA Ops:
  0.6 101.1 %attention.1 = (bf16[384,1536]{1,0:T(8,128)(2,1)}, bf16[384,1536]{1,0:T(8,128)(2,1)}, bf16[384,1536]{1,0:T(8,128)(2,1)}, f32[2,12,128]{2,1,0:T(8,128)}) custom-call(s32[3]{0:T(128)} %bitcast.23, bf16[384,1536]{1,0:T(8,128)(2,1)} %bitcast.14, bf16[384,1536]{1,0:T(8,128)(2,1)} %bitcast.15, bf16[384,1536]{1,0:T(8,128)(2,1)} %bitcast.16, ...), custom_call_target="tpu_custom_call" | custom-call | tf_op jit(solution)/shard_map/attention/pallas_call | solution.py:392
  101.7 1.3 %slice_bitcast_fusion = (f32[1536]{0:T(1024)}, f32[1536]{0:T(1024)}) fusion(f32[2,12,128]{2,1,0:T(8,128)} %get-tuple-element.12), kind=kLoop, calls=%fused_computation | loop fusion | bytes 24576 | tf_op jit(solution)/shard_map/reshape;squeeze | solution.py:445
  103.0 0.0 copy-start.1
  103.0 2.5 %copy.15 = bf16[1,384,1536]{2,1,0:T(8,128)(2,1)} copy(bf16[1,384,1536]{2,1,0:T(8,128)(2,1)} %bitcast.20) | data formatting | bytes 2359296
  105.5 0.0 copy-done.1
  105.5 0.0 copy-start
  105.5 1.0 copy.16
  106.5 0.7 copy-done
  107.2 1.0 copy.17
Async XLA Ops:
  103.0 2.5 %copy-start.1 = (bf16[384,1536]{1,0:T(8,128)(2,1)S(1)}, bf16[384,1536]{1,0:T(8,128)(2,1)}, u32[]{:S(2)}) copy-start(bf16[384,1536]{1,0:T(8,128)(2,1)} %get-tuple-element.10) | copy-start | bytes 3538948
  105.5 1.7 %copy-start = (bf16[384,1536]{1,0:T(8,128)(2,1)S(1)}, bf16[384,1536]{1,0:T(8,128)(2,1)}, u32[]{:S(2)}) copy-start(bf16[384,1536]{1,0:T(8,128)(2,1)} %get-tuple-element.11) | copy-start | bytes 3538948
